TPU v7x, 256 devices: a whole 4x4x8 slice. The times are simulated.
256 devices in a mesh: sens: 16 (over y, x), pts: 16 (over z, core).
Axes of the slice: x: 4, y: 4, z: 8, core: 2. Of those that a mesh axis runs over, the one named last changes fastest.
Arguments:
- records: float32 [4, 640, 383], P(None, 'sens'), may hold values from -8 to 8
- tiles: bfloat16 [2, 640, 1024, 384], P(None, 'sens', 'pts'), may hold values from -6 to 6
- gauge_response_blocks: bfloat16 [2, 64, 1024, 384], P(None, 'sens', 'pts'), may hold values from -6 to 6
- prior: float32 [1024, 384], P('pts'), may hold values from 0.1 to 1
- noise: float32 [640], P('sens'), may hold values from 0.2 to 1
Outputs:
- krylov_estimate: float32 [4, 640, 383], P(None, 'sens')
- predicted_wave_records: float32 [4, 64, 383], P(None, 'sens')
All inputs are finite; a program needn't handle non-finite values.
Results may differ from a plain program's by a relative error of at most 0.0059.
Values may be sent and summed in bfloat16 or wider, within the bound.
No kernel may reach another device: no remote copies, remote signals or barrier semaphores. Data moves between devices by JAX's collectives and lax.ppermute only.
A program may use at most 128 MiB of HBM per device.

v0:
```python
import math

import jax
import jax.numpy as jnp
from jax import lax
from jax.sharding import PartitionSpec as P

ITERS = 2


def tables(steps, freqs_count, padded):
    times = jnp.arange(steps, dtype=jnp.int32)
    freqs = jnp.arange(freqs_count, dtype=jnp.int32)
    phase = times[:, None] * freqs[None, :] % padded
    angle = phase.astype(jnp.float32) * (2.0 * math.pi / padded)
    edge = (freqs == 0) | (freqs == padded // 2)
    weights = jnp.where(edge, 1.0, 2.0).astype(jnp.float32) / padded
    return (jnp.cos(angle) * weights[None, :], jnp.sin(angle) * weights[None, :])


def analyze(series, even_harmonic_term, odd_harmonic_term):
    real_part = jnp.einsum(
        "bst,tf->bsf", series, even_harmonic_term, precision=lax.Precision.HIGHEST
    )
    imaginary_part = -jnp.einsum(
        "bst,tf->bsf", series, odd_harmonic_term, precision=lax.Precision.HIGHEST
    )
    return jnp.stack([real_part, imaginary_part]).astype(jnp.bfloat16)


def synthesize(real_part, imaginary_part, even_harmonic_term, odd_harmonic_term):
    first = jnp.einsum(
        "bsf,tf->bst", real_part, even_harmonic_term, precision=lax.Precision.HIGHEST
    )
    second = jnp.einsum(
        "bsf,tf->bst", imaginary_part, odd_harmonic_term, precision=lax.Precision.HIGHEST
    )
    return first - second


def adjoint_local(spectra, tiles):
    real_part = jnp.einsum("cbsf,cspf->bpf", spectra, tiles, preferred_element_type=jnp.float32)
    swapped = jnp.stack([spectra[1], -spectra[0]])
    imaginary_part = jnp.einsum(
        "cbsf,cspf->bpf", swapped, tiles, preferred_element_type=jnp.float32
    )
    return jnp.stack([real_part, imaginary_part])


def weigh(series, tiles, prior, even_harmonic_term, odd_harmonic_term):
    partial_points = adjoint_local(analyze(series, even_harmonic_term, odd_harmonic_term), tiles)
    total = lax.psum(partial_points, "sens")
    return (total * prior[None, None, :, :]).astype(jnp.bfloat16)


def map_onto_gauges(weighted, tiles, even_harmonic_term, odd_harmonic_term):
    first_pair = jnp.stack([weighted[0], -weighted[1]])
    second_pair = jnp.stack([weighted[1], weighted[0]])
    real_part = jnp.einsum("cbpf,crpf->brf", first_pair, tiles, preferred_element_type=jnp.float32)
    imaginary_part = jnp.einsum(
        "cbpf,crpf->brf", second_pair, tiles, preferred_element_type=jnp.float32
    )
    real_part, imaginary_part = lax.psum((real_part, imaginary_part), "pts")
    return synthesize(real_part, imaginary_part, even_harmonic_term, odd_harmonic_term)


def on_device(records, tiles, gauge_response_blocks, prior, noise):
    steps = records.shape[2]
    even_harmonic_term, odd_harmonic_term = tables(steps, prior.shape[1], 2 * steps)

    def squares(residual):
        return lax.psum(jnp.sum(residual * residual, axis=(1, 2)), "sens")

    krylov_estimate = jnp.zeros_like(records)
    residual = records
    direction = records
    norm_now = squares(residual)
    for step in range(ITERS):
        covariance_weighted = weigh(direction, tiles, prior, even_harmonic_term, odd_harmonic_term)
        image = (
            map_onto_gauges(covariance_weighted, tiles, even_harmonic_term, odd_harmonic_term)
            + noise[None, :, None] * direction
        )
        alpha = norm_now / lax.psum(jnp.sum(direction * image, axis=(1, 2)), "sens")
        krylov_estimate = krylov_estimate + alpha[:, None, None] * direction
        residual = residual - alpha[:, None, None] * image
        norm_next = squares(residual)
        direction = residual + (norm_next / norm_now)[:, None, None] * direction
        norm_now = norm_next
    weighted = weigh(krylov_estimate, tiles, prior, even_harmonic_term, odd_harmonic_term)
    predicted_wave_records = map_onto_gauges(
        weighted, gauge_response_blocks, even_harmonic_term, odd_harmonic_term
    )
    return (krylov_estimate, predicted_wave_records)


def solution(mesh):
    return jax.shard_map(
        on_device,
        mesh=mesh,
        in_specs=(
            P(None, "sens", None),
            P(None, "sens", "pts", None),
            P(None, "sens", "pts", None),
            P("pts", None),
            P("sens"),
        ),
        out_specs=(P(None, "sens", None), P(None, "sens", None)),
        check_vma=False,
    )
```

profile of v0, /device:TPU:1, one launch (start us, length us, event | category | flops | bytes accessed | tf_op | source)
XLA Modules:
  0.0 811.3 jit_solution(9402701455974305575)
XLA Ops:
  7.2 3.9 fusion.151
  11.2 2.9 fusion.12
  14.2 0.7 copy.9
  14.9 14.0 %copy.8 = bf16[2,40,64,384]{2,1,0,3:T(8,128)(2,1)} copy(bf16[2,40,64,384]{3,2,1,0:T(8,128)(2,1)} %param.6) | data formatting | bytes 7864320 | tf_op args[1]
  29.7 4.9 convolution_bitcast_fusion.4
  35.2 2.6 convolution_bitcast_fusion.5
  37.8 1.6 pad_maximum_fusion
  39.7 10.6 %copy.22 = bf16[2,40,64,384]{2,1,3,0:T(8,128)(2,1)} copy(bf16[2,40,64,384]{3,2,1,0:T(8,128)(2,1)} %param.6) | data formatting | bytes 7864320 | tf_op args[1]
  50.5 90.5 %all-reduce.10.cloned.1.call-done = f32[2,4,64,384]{2,1,3,0:T(4,128)} async-done(((f32[2,4,64,384]{2,1,3,0:T(4,128)}), f32[2,4,64,384]{2,1,3,0:T(4,128)}) %all-reduce.10.cloned.1.call-update) | async-done | bytes 786448 | tf_op jit(solution)/shard_map/psum | solution.py:52
  140.9 1.7 multiply_convert_fusion.2
  143.1 5.3 fusion.17
  148.5 1.0 copy.24
  149.5 5.3 fusion.13
  154.8 1.0 copy.23
  155.9 110.7 %all-reduce.18.cloned.1.call-done = (f32[4,40,384]{2,1,0:T(8,128)}, f32[4,40,384]{2,1,0:T(8,128)}) async-done(((f32[4,40,384]{2,1,0:T(8,128)}, f32[4,40,384]{2,1,0:T(8,128)}), (f32[4,40,384]{2,1,0:T(8,128)}, f32[4,40,384]{2,1,0:T(8,128)})) %all-reduce.18.cloned.1.call-update) | async-done | bytes 491536 | tf_op jit(solution)/shard_map/psum | solution.py:63
  266.6 4.0 fusion.51
  270.6 3.2 multiply_reduce_fusion.1
  273.7 33.2 %all-reduce.3 = (f32[4]{0:T(128)S(1)}, f32[4]{0:T(128)S(1)}) all-reduce(f32[4]{0:T(128)S(1)} %get-tuple-element.3, f32[4]{0:T(128)S(1)} %get-tuple-element.2), channel_id=1, replica_groups=mesh['sens'=16,'pts'=16] {'sens'}, use_global_device_ids=true, to_apply=%region_1.2 | all-reduce | flops 8 | bytes 64 | tf_op jit(solution)/shard_map/psum | solution.py:72
  307.1 28.9 %psum.96 = f32[4]{0:T(128)S(1)} all-reduce(f32[4]{0:T(128)S(1)} %multiply_reduce_fusion), channel_id=1, replica_groups=mesh['sens'=16,'pts'=16] {'sens'}, use_global_device_ids=true, to_apply=%region_8.9 | all-reduce | flops 4 | bytes 32 | tf_op jit(solution)/shard_map/psum | solution.py:72
  336.1 2.9 fusion.152
  339.0 2.9 fusion.11
  342.8 4.7 convolution_bitcast_fusion.3
  348.3 4.7 convolution_bitcast_fusion.2
  353.0 1.6 pad_maximum_fusion.1
  354.8 108.5 %all-reduce.12.cloned.1.call-done = f32[2,4,64,384]{2,1,3,0:T(4,128)} async-done(((f32[2,4,64,384]{2,1,3,0:T(4,128)}), f32[2,4,64,384]{2,1,3,0:T(4,128)}) %all-reduce.12.cloned.1.call-update) | async-done | bytes 786448 | tf_op jit(solution)/shard_map/psum | solution.py:52
  463.3 1.7 multiply_convert_fusion.1
  465.5 5.3 fusion.25
  470.8 1.0 copy.28
  471.8 5.3 fusion.21
  477.2 1.0 copy.27
  478.2 110.7 %all-reduce.16.cloned.1.call-done = (f32[4,40,384]{2,1,0:T(8,128)}, f32[4,40,384]{2,1,0:T(8,128)}) async-done(((f32[4,40,384]{2,1,0:T(8,128)}, f32[4,40,384]{2,1,0:T(8,128)}), (f32[4,40,384]{2,1,0:T(8,128)}, f32[4,40,384]{2,1,0:T(8,128)})) %all-reduce.16.cloned.1.call-update) | async-done | bytes 491536 | tf_op jit(solution)/shard_map/psum | solution.py:63
  588.9 4.0 fusion.48
  592.9 3.1 fusion.6
  596.1 33.4 %psum.100 = f32[4]{0:T(128)S(1)} all-reduce(f32[4]{0:T(128)S(1)} %fusion.6), channel_id=1, replica_groups=mesh['sens'=16,'pts'=16] {'sens'}, use_global_device_ids=true, to_apply=%region_13.14 | all-reduce | flops 4 | bytes 32 | tf_op jit(solution)/shard_map/psum | solution.py:84
  629.6 2.9 fusion.153
  632.5 2.9 fusion.10
  635.5 0.7 copy.16
  636.2 4.7 convolution_bitcast_fusion.1
  641.0 0.7 copy.18
  641.7 4.7 convolution_bitcast_fusion
  646.5 1.6 pad_maximum_fusion.2
  648.0 1.0 copy-done.2
  649.0 0.8 copy.31
  649.8 98.4 %all-reduce.14.cloned.1.call-done = f32[2,4,64,384]{2,1,3,0:T(4,128)} async-done(((f32[2,4,64,384]{2,1,3,0:T(4,128)}), f32[2,4,64,384]{2,1,3,0:T(4,128)}) %all-reduce.14.cloned.1.call-update) | async-done | bytes 786448 | tf_op jit(solution)/shard_map/psum | solution.py:52
  748.3 1.7 multiply_convert_fusion
  752.3 45.6 %all-reduce = (f32[4,4,384]{2,1,0:T(4,128)S(1)}, f32[4,4,384]{2,1,0:T(4,128)S(1)}) all-reduce(f32[4,4,384]{2,1,0:T(4,128)S(1)} %bitcast.145, f32[4,4,384]{2,1,0:T(4,128)S(1)} %bitcast.144), channel_id=1, replica_groups=mesh['sens'=16,'pts'=16] {'pts'}, use_global_device_ids=true, to_apply=%region_15.16 | all-reduce | flops 12288 | bytes 98304 | tf_op jit(solution)/shard_map/psum | solution.py:63
  797.9 2.9 fusion.45
  800.8 3.5 convolution_subtract_fusion.2
  (46 shorter events, 7.3 us)
Async XLA Ops:
  7.2 4.0 copy-start.1
  7.2 133.8 %all-reduce.10.cloned.1.call-start = ((), (), s32[]{:S(2)}) async-start(), calls=%async_computation | async-start | bytes 3145728 | tf_op jit(solution)/shard_map/psum | solution.py:52
  29.7 5.6 copy-start
  39.5 10.9 %copy-start.4 = (f32[64,384]{1,0:T(8,128)S(1)}, f32[64,384]{1,0:T(8,128)}, u32[]{:S(2)}) copy-start(f32[64,384]{1,0:T(8,128)} %param.8) | copy-start | bytes 294916
  39.5 227.1 %all-reduce.18.cloned.1.call-start = ((), (), s32[]{:S(2)}) async-start(), calls=%async_computation.4 | async-start | bytes 983040 | tf_op jit(solution)/shard_map/psum | solution.py:63
  154.8 115.8 %copy-start.7 = (f32[40]{0:T(128)S(1)}, f32[40]{0:T(128)}, u32[]{:S(2)}) copy-start(f32[40]{0:T(128)} %param.9) | copy-start | bytes 484
  155.8 307.5 %all-reduce.12.cloned.1.call-start = ((), (), s32[]{:S(2)}) async-start(), calls=%async_computation.1 | async-start | bytes 3145728 | tf_op jit(solution)/shard_map/psum | solution.py:52
  266.6 4.0 copy-start.5
  354.6 234.3 %all-reduce.16.cloned.1.call-start = ((), (), s32[]{:S(2)}) async-start(), calls=%async_computation.3 | async-start | bytes 983040 | tf_op jit(solution)/shard_map/psum | solution.py:63
  478.2 270.1 %all-reduce.14.cloned.1.call-start = ((), (), s32[]{:S(2)}) async-start(), calls=%async_computation.2 | async-start | bytes 3145728 | tf_op jit(solution)/shard_map/psum | solution.py:52
  588.9 4.0 copy-start.6
  629.5 5.9 copy-start.3
  648.0 1.0 copy-start.2
Sparse Core Ops, SparseCore 0:
  39.6 101.3 all-reduce.9
  155.9 110.5 all-reduce.17
  354.7 108.5 all-reduce.11
  478.3 110.5 all-reduce.15
  648.2 100.0 all-reduce.13
where the time goes:
time: 822 us; the launch traced here: 811 us
  waiting for transfers between devices  519 us (63%)
  blocking collectives  141 us (17%)
  matrix products  88.3 us (11%)
  local copies, waits for them, and re-layouts  36.1 us (4%)
  between operations  14.6 us (2%)
  other arithmetic  11.8 us (1%)
    psum x3, waiting for transfers between devices, weigh(): total = lax.psum(partial_points, 'sens')  297 us
    psum x2, waiting for transfers between devices, map_onto_gauges(): real_part, imaginary_part = lax.psum((real_part, imaginary_part), 'pts')  221 us
    psum x2, blocking collectives, squares(): return lax.psum(jnp.sum(residual * residual, axis=(1, 2)), 'sens')  62.1 us
    psum x1, blocking collectives, map_onto_gauges(): real_part, imaginary_part = lax.psum((real_part, imaginary_part), 'pts')  45.6 us
    psum x1, blocking collectives, on_device(): alpha = norm_now / lax.psum(jnp.sum(direction * image, axis=(1, 2)), 'sens')  33.4 us
    unnamed x20, local copies, waits for them, and re-layouts  27.2 us
  transfers between devices with their start and end apart: 5, of which 5 were waited for; matrix products, arithmetic and copies ran while one was open for 1% of the time, Pallas kernels for 0%

commit v1 on v0

v1 whole, which is shorter than its diff:
```python
import functools

import jax
import jax.numpy as jnp
import numpy as np
from jax import lax
from jax.experimental import pallas as pl
from jax.experimental.pallas import tpu as pltpu
from jax.sharding import Mesh
from jax.sharding import PartitionSpec as P

SENS = ("y", "x")
PTS = ("z", "core")
REALS = 4
LANES = 128
BAND = 32
EXTRA = 16
F32 = jnp.float32
BF16 = jnp.bfloat16
VMEM = pl.BlockSpec(memory_space=pltpu.VMEM)
SMEM = pl.BlockSpec(memory_space=pltpu.SMEM)


def make_tables(freqs):
    padded = 2 * (freqs - 1)
    steps = np.arange(freqs, dtype=np.int64)
    angle = (steps[:, None] * steps[None, :] % padded) * (2.0 * np.pi / padded)
    both = np.concatenate([np.cos(angle), -np.sin(angle)], axis=1)
    high = both.astype(BF16)
    low = (both - high.astype(np.float64)).astype(BF16)
    weights = np.where((steps == 0) | (steps == freqs - 1), 1.0, 2.0) / padded
    weights = np.tile(weights[None], (8, 2)).astype(np.float32)
    return jnp.asarray(high), jnp.asarray(low), jnp.asarray(weights)


def product(left, high, low):
    first = left.astype(BF16)
    second = (left - first.astype(F32)).astype(BF16)

    def dot(a, b):
        return jnp.dot(a, b, preferred_element_type=F32)

    return dot(first, high) + (dot(first, low) + dot(second, high))


def lane_of(shape):
    return lax.broadcasted_iota(jnp.int32, shape, len(shape) - 1)


def three(values):
    first = values.astype(BF16).astype(F32)
    rest = values - first
    second = rest.astype(BF16).astype(F32)
    return first, second, rest - second


def write_scalars(out, columns):
    lane = lane_of((8, LANES))
    tile = jnp.zeros((8, LANES), F32)
    for k, column in enumerate(columns):
        tile = jnp.where(lane == k, column, tile)
    first, second, third = three(tile)
    tile = first + pltpu.roll(second, 32, 1) + pltpu.roll(third, 64, 1)
    block = jnp.concatenate([tile, jnp.zeros_like(tile)]).astype(BF16)
    rows = out.shape[1] - EXTRA
    for k in range(out.shape[0]):
        out[k, rows:, :] = block


def band_sum(first, second, start, count):
    total = jnp.zeros((8, first.shape[1]), F32)
    for row in range(start, start + count, 8):
        total = total + first[row : row + 8, :] * second[row : row + 8, :]
    return jnp.sum(total, axis=1, keepdims=True)


def send_points(series, tiles, high, low, weights, spec, out):
    sens, points, freqs = tiles.shape[1:]
    spec[...] = product(series[...], high[...], low[...]) * weights[0:1, :]
    blocks = freqs // LANES

    def part(index, _):
        band = index // blocks
        block = index % blocks
        lanes = pl.ds(pl.multiple_of(block * LANES, LANES), LANES)
        sines = pl.ds(pl.multiple_of(freqs + block * LANES, LANES), LANES)
        range_ = pl.ds(pl.multiple_of(band * BAND, BAND), BAND)

        def group(g, acc):
            acc = list(acc)
            rows = [pl.ds(pl.multiple_of(b * sens + g * 8, 8), 8) for b in range(REALS)]
            real = [spec[r, lanes] for r in rows]
            imag = [spec[r, sines] for r in rows]
            for j in range(8):
                tr = tiles[0, g * 8 + j, range_, lanes].astype(F32)
                ti = tiles[1, g * 8 + j, range_, lanes].astype(F32)
                for b in range(REALS):
                    sr = real[b][j : j + 1]
                    si = imag[b][j : j + 1]
                    re, im = acc[b]
                    acc[b] = (re + (sr * tr + si * ti), im + (si * tr - sr * ti))
            return tuple(acc)

        zero = jnp.zeros((BAND, LANES), F32)
        acc = lax.fori_loop(0, sens // 8, group, ((zero, zero),) * REALS)
        parts = points // BAND
        rows = pl.ds(pl.multiple_of(block * BAND, BAND), BAND)
        for b in range(REALS):
            for c in range(2):
                out[(c * REALS + b) * parts + band, rows, :] = acc[b][c].astype(BF16)
        return 0

    lax.fori_loop(0, (points // BAND) * blocks, part, 0)


def first_kernel(series, noise, tiles, high, low, weights, out, spec, *, sens):
    values = series[...]
    noisy = values * noise[...]
    columns = [band_sum(values, values, b * sens, sens) for b in range(REALS)]
    columns += [band_sum(values, noisy, b * sens, sens) for b in range(REALS)]
    write_scalars(out, columns)
    send_points(series, tiles, high, low, weights, spec, out)


def second_kernel(
    core, mine, theirs, series, noise, begin, tiles, high, low, weights, out, residual, alpha, image, spec
):
    half, freqs = mine.shape
    sens = 2 * half // REALS
    image[pl.ds(pl.multiple_of(core[0] * half, 8), half), :] = mine[...]
    image[pl.ds(pl.multiple_of((1 - core[0]) * half, 8), half), :] = theirs[...]
    lane = lane_of((8, LANES))
    tile = jnp.zeros((8, LANES), F32)
    real = lane_of((sens, freqs)) < freqs - 1
    last = freqs - 1
    columns = [[], [], []]
    for b in range(REALS):
        energy = image[b : b + 1, last:] + image[8 + b : 9 + b, last:] + image[16 + b : 17 + b, last:]
        scale = begin[0:1, b : b + 1] / (energy + begin[0:1, REALS + b : REALS + b + 1])
        tile = jnp.where(lane == b, scale, tile)
        rows = slice(b * sens, (b + 1) * sens)
        values = series[rows, :]
        noisy = noise[rows, :]
        left = values - scale * (jnp.where(real, image[rows, :], 0.0) + noisy * values)
        residual[rows, :] = left
        columns[0].append(band_sum(left, left, 0, sens))
        columns[1].append(band_sum(left, left * noisy, 0, sens))
        columns[2].append(band_sum(left, values * noisy, 0, sens))
    alpha[...] = tile
    write_scalars(out, columns[0] + columns[1] + columns[2])
    send_points(residual, tiles, high, low, weights, spec, out)


def sum_message(got):
    rows = got.shape[1] - EXTRA
    total = got[0, :rows, :].astype(F32)
    extra = got[0, rows:, :].astype(F32)
    for k in range(1, got.shape[0]):
        total = total + got[k, :rows, :].astype(F32)
        extra = extra + got[k, rows:, :].astype(F32)
    sums = jnp.broadcast_to(jnp.sum(extra, axis=0, keepdims=True), (8, LANES))
    sums = sums + pltpu.roll(sums, LANES - 32, 1) + pltpu.roll(sums, LANES - 64, 1)
    return total, sums


def put_weighted(total, prior, out):
    for block in range(prior.shape[1] // LANES):
        rows = slice(block * BAND, (block + 1) * BAND)
        lanes = slice(block * LANES, (block + 1) * LANES)
        part = (total[rows] * prior[:, lanes]).astype(BF16)
        for k in range(out.shape[0]):
            out[k, rows, :] = part


def weigh_kernel(got, prior, out, kept, sums_out):
    total, sums = sum_message(got)
    kept[...] = total
    sums_out[...] = sums
    put_weighted(total, prior, out)


def weigh_next_kernel(got, prior, before, begin, pick, out, sums_out):
    total, sums = sum_message(got)
    sums_out[...] = sums
    lane = lane_of((8, LANES))
    ratio = sums / jnp.where(lane < REALS, begin[...], 1.0)
    beta = jnp.sum(jnp.where(lane == pick[0], ratio, 0.0), axis=1, keepdims=True)[0:1]
    put_weighted(total + beta * before[...], prior, out)


def widen(weighted, prior, wide):
    energy = [jnp.zeros((8, LANES), F32)] * REALS
    parts = weighted.shape[0] // (2 * REALS)
    for h in range(parts):
        for block in range(prior.shape[1] // LANES):
            for row in range(0, BAND, 16):
                lanes = slice(block * LANES, (block + 1) * LANES)
                inverse = 1.0 / prior[h * BAND + row : h * BAND + row + 16, lanes]
                for b in range(REALS):
                    for c in range(2):
                        k = (c * REALS + b) * parts + h
                        at = slice(block * BAND + row, block * BAND + row + 16)
                        part = weighted[k, at, :].astype(F32)
                        wide[k, at, :] = part
                        term = part * part * inverse
                        energy[b] = energy[b] + (term[:8] + term[8:])
    return [
        jnp.sum(jnp.sum(e, axis=0, keepdims=True), axis=1, keepdims=True) for e in energy
    ]


def merge(first, second, width, place):
    low = (place & width) == 0
    other = jnp.where(low, second, first)
    if width == 4:
        other = pltpu.roll(other, 4, 0)
    else:
        other = jnp.where(low, pltpu.roll(other, 8 - width, 0), pltpu.roll(other, width, 0))
    return jnp.where(low, first, second) + other


def site_sums(tiles, wide, sites, reals, block, lanes):
    sums = {}
    for p in range(0, tiles.shape[2], 16):
        h, row = divmod(p, BAND)
        pair = [[tiles[c, s, pl.ds(p, 16), lanes].astype(F32) for c in range(2)] for s in sites]
        for q in (0, 8):
            for b in reals:
                at = pl.ds(pl.multiple_of(block * BAND + row + q, 8), 8)
                parts = tiles.shape[2] // BAND
                wr = wide[b * parts + h, at, :]
                wi = wide[(REALS + b) * parts + h, at, :]
                for j in range(len(sites)):
                    tr = pair[j][0][q : q + 8]
                    ti = pair[j][1][q : q + 8]
                    re = wr * tr - wi * ti
                    im = wr * ti + wi * tr
                    if (j, b) in sums:
                        re = sums[j, b][0] + re
                        im = sums[j, b][1] + im
                    sums[j, b] = (re, im)
    return sums


def synthesize(rows, weights, high, low, energy, stride):
    count, freqs = rows.shape[0], rows.shape[1] // 2
    scaled = rows[...] * weights[0:1, :]
    series = product(scaled[:, :freqs], high[:, :freqs], low[:, :freqs]) + product(
        scaled[:, freqs:], high[:, freqs:], low[:, freqs:]
    )
    row = lax.broadcasted_iota(jnp.int32, (count, freqs), 0)
    lane = lane_of((count, freqs))
    carried = jnp.zeros((count, 1), F32)
    index = row[:, 0:1]
    for b in range(REALS):
        hit = (index % stride == b) & (index < 3 * stride)
        carried = jnp.where(hit, energy[b], carried)
    return jnp.where(lane == freqs - 1, carried, series)


def forward_kernel(core, weighted, prior, tiles, high, low, weights, mine, other, wide, rows, full):
    sens, points, freqs = tiles.shape[1:]
    energy = widen(weighted, prior, wide)
    place = lax.broadcasted_iota(jnp.int32, (8, LANES), 0)
    blocks = freqs // LANES

    def part(index, _):
        g = index // blocks
        block = index % blocks
        lanes = pl.ds(pl.multiple_of(block * LANES, LANES), LANES)
        sines = pl.ds(pl.multiple_of(freqs + block * LANES, LANES), LANES)

        def pair(k):
            sums = site_sums(tiles, wide, [g * 8 + k, g * 8 + k + 4], range(REALS), block, lanes)
            return [
                [merge(sums[0, b][c], sums[1, b][c], 4, place) for c in range(2)]
                for b in range(REALS)
            ]

        def both(k):
            first = pair(k)
            second = pair(k + 2)
            return [
                [merge(first[b][c], second[b][c], 2, place) for c in range(2)]
                for b in range(REALS)
            ]

        first = both(0)
        second = both(1)
        for b in range(REALS):
            at = pl.ds(pl.multiple_of(b * sens + g * 8, 8), 8)
            rows[at, lanes] = merge(first[b][0], second[b][0], 1, place)
            rows[at, sines] = merge(first[b][1], second[b][1], 1, place)
        return 0

    lax.fori_loop(0, (sens // 8) * blocks, part, 0)
    half = REALS * sens // 2
    series = synthesize(rows, weights, high, low, energy + energy, 8)
    row = lax.broadcasted_iota(jnp.int32, (half, freqs), 0)
    lane = lane_of((half, freqs))
    carried = series[:half, freqs - 1 :]
    full[:half, :] = series[:half]
    full[half:, :] = jnp.where(lane == freqs - 1, carried, series[half:])
    mine[...] = full[pl.ds(pl.multiple_of(core[0] * half, 8), half), :]
    other[...] = full[pl.ds(pl.multiple_of((1 - core[0]) * half, 8), half), :]


def site_kernel(weighted, prior, tiles, high, low, weights, out, wide, rows):
    freqs = tiles.shape[3]
    energy = widen(weighted, prior, wide)
    place = lax.broadcasted_iota(jnp.int32, (8, LANES), 0)

    def part(block, _):
        lanes = pl.ds(pl.multiple_of(block * LANES, LANES), LANES)
        sines = pl.ds(pl.multiple_of(freqs + block * LANES, LANES), LANES)
        for low_b in range(0, REALS, 2):
            sums = site_sums(tiles, wide, range(4), (low_b, low_b + 1), block, lanes)
            for c, where in ((0, lanes), (1, sines)):
                blocks = [sums[j, low_b + b][c] for b in range(2) for j in range(4)]
                for width in (4, 2, 1):
                    half = len(blocks) // 2
                    blocks = [
                        merge(x, y, width, place) for x, y in zip(blocks[:half], blocks[half:])
                    ]
                rows[pl.ds(low_b * 4, 8), where] = blocks[0]
        return 0

    lax.fori_loop(0, freqs // LANES, part, 0)
    out[...] = synthesize(rows, weights, high, low, energy, REALS)


def spread_kernel(mine, got, out, *, stride, begin):
    values = mine[...] + got[...]
    count, freqs = values.shape
    row = lax.broadcasted_iota(jnp.int32, (count, freqs), 0) - begin
    carried = lane_of((count, freqs)) == freqs - 1
    _, second, third = three(values)
    second_row = (row >= stride) & (row < 2 * stride)
    third_row = (row >= 2 * stride) & (row < 3 * stride)
    values = jnp.where(carried & second_row, second, values)
    values = jnp.where(carried & third_row, third, values)
    block = values.astype(BF16)
    for k in range(out.shape[0]):
        out[k] = block


def sum_kernel(got, out):
    total = got[0].astype(F32)
    for k in range(1, got.shape[0]):
        total = total + got[k].astype(F32)
    out[...] = total


def last_kernel(got, begin, later, alpha, series, residual, estimate, predicted):
    reals, sens, steps = estimate.shape
    sites = predicted.shape[1]
    count = reals * sites
    total = got[0].astype(F32)
    for k in range(1, got.shape[0]):
        total = total + got[k].astype(F32)
    last = total.shape[1] - 1
    for b in range(reals):
        rows = [count + k * reals + b for k in range(3)]
        energy = sum(total[r : r + 1, last:] for r in rows)

        def value(ref, kind):
            return ref[0:1, kind * reals + b : kind * reals + b + 1]

        beta = value(later, 0) / value(begin, 0)
        curve = energy + value(later, 1) + 2.0 * beta * value(later, 2)
        curve = curve + beta * beta * value(begin, 1)
        first = value(alpha, 0)
        second = value(later, 0) / curve
        at = slice(b * sens, (b + 1) * sens)
        values = series[at, :]
        result = first * values + second * (residual[at, :] + beta * values)
        estimate[b] = result[:, :steps]
        low = total[b * sites : (b + 1) * sites]
        high = total[count + b * sites : count + (b + 1) * sites]
        predicted[b] = (first * low + second * high)[:, :steps]


def call(kernel, name, outs, scratch, specs, *args):
    return pl.pallas_call(
        kernel,
        in_specs=specs,
        out_specs=[VMEM] * len(outs),
        out_shape=[jax.ShapeDtypeStruct(*out) for out in outs],
        scratch_shapes=[pltpu.VMEM(*one) for one in scratch],
        compiler_params=pltpu.CompilerParams(vmem_limit_bytes=24 * 2**20),
        name=name,
    )(*args)


def on_device(records, tiles, gauges, prior, noise):
    reals, sensors, steps = records.shape
    points, freqs = prior.shape
    sites = gauges.shape[1]
    tables = make_tables(freqs)
    senders = lax.axis_size("y") * lax.axis_size("x")
    heights = lax.axis_size("z")
    place = lax.axis_index("y") * lax.axis_size("x") + lax.axis_index("x")
    core = lax.axis_index("core").astype(jnp.int32).reshape(1)
    start = lax.rem(place * BAND, points)
    prior_chunk = lax.dynamic_slice(prior, (start, 0), (BAND, freqs))
    pick = lax.rem(place * BAND // points, reals).astype(jnp.int32).reshape(1)
    count = reals * sensors
    half = count // 2
    series = jnp.pad(records, ((0, 0), (0, 0), (0, freqs - steps))).reshape(count, freqs)
    noisy = jnp.broadcast_to(noise[None, :], (reals, sensors)).reshape(count, 1)
    block_rows = BAND * freqs // LANES
    message = ((senders, block_rows + EXTRA, LANES), BF16)
    weighted_shape = (senders, block_rows, LANES)
    spectra = ((count, 2 * freqs), F32)
    rows = ((count, freqs), F32)
    tile = ((8, LANES), F32)

    def swap(block):
        return lax.ppermute(block, "core", [(0, 1), (1, 0)])

    (sent,) = call(
        functools.partial(first_kernel, sens=sensors),
        "first",
        [message],
        [spectra],
        [VMEM] * 6,
        *(series, noisy, tiles, *tables),
    )
    got = lax.all_to_all(sent, SENS, 0, 0)
    sent, points_0, begin = call(
        weigh_kernel,
        "weigh",
        [(weighted_shape, BF16), ((block_rows, LANES), F32), tile],
        [],
        [VMEM] * 2,
        *(got, prior_chunk),
    )
    weighted_0 = lax.all_to_all(sent, SENS, 0, 0)
    mine, other = call(
        forward_kernel,
        "forward",
        [((half, freqs), F32)] * 2,
        [(weighted_shape, F32), spectra, rows],
        [SMEM] + [VMEM] * 6,
        *(core, weighted_0, prior, tiles, *tables),
    )
    (sent,) = call(
        functools.partial(spread_kernel, stride=8, begin=0),
        "spread",
        [((heights, half, freqs), BF16)],
        [],
        [VMEM] * 2,
        *(mine, swap(other)),
    )
    got = lax.all_to_all(sent, "z", 0, 0)
    (mine,) = call(sum_kernel, "gather", [((half, freqs), F32)], [], [VMEM], got)
    theirs = swap(mine)
    sent, residual, alpha = call(
        second_kernel,
        "second",
        [message, rows, tile],
        [rows, spectra],
        [SMEM] + [VMEM] * 9,
        *(core, mine, theirs, series, noisy, begin, tiles, *tables),
    )
    got = lax.all_to_all(sent, SENS, 0, 0)
    sent, later = call(
        weigh_next_kernel,
        "weigh_next",
        [(weighted_shape, BF16), tile],
        [],
        [VMEM] * 4 + [SMEM],
        *(got, prior_chunk, points_0, begin, pick),
    )
    weighted_1 = lax.all_to_all(sent, SENS, 0, 0)

    def site(weighted, name):
        return call(
            site_kernel,
            name,
            [((reals * sites, freqs), F32)],
            [(weighted_shape, F32), ((reals * sites, 2 * freqs), F32)],
            [VMEM] * 6,
            *(weighted, prior, gauges, *tables),
        )[0]

    block = jnp.concatenate([site(weighted_0, "site_0"), site(weighted_1, "site_1")])
    (sent,) = call(
        functools.partial(spread_kernel, stride=reals, begin=reals * sites),
        "spread_sites",
        [((heights,) + block.shape, BF16)],
        [],
        [VMEM] * 2,
        *(block, swap(block)),
    )
    got = lax.all_to_all(sent, "z", 0, 0)
    estimate, predicted = call(
        last_kernel,
        "last",
        [((reals, sensors, steps), F32), ((reals, sites, steps), F32)],
        [],
        [VMEM] * 6,
        *(got, begin, later, alpha, series, residual),
    )
    return (estimate, predicted)


def solution(mesh):
    fine = Mesh(mesh.devices.reshape(4, 4, 8, 2), SENS + PTS)
    return jax.shard_map(
        on_device,
        mesh=fine,
        in_specs=(
            P(None, SENS, None),
            P(None, SENS, PTS, None),
            P(None, SENS, PTS, None),
            P(PTS, None),
            P(SENS),
        ),
        out_specs=(P(None, SENS, None), P(None, SENS, None)),
        check_vma=False,
    )
```

time: 822 us -> 135 us (0.16); the launches traced: 811 us -> 134 us
  waiting for transfers between devices: 519 us -> 38.7 us
  blocking collectives: 141 us -> 36.5 us
  matrix products: 88.3 us -> 0 us
  local copies, waits for them, and re-layouts: 36.1 us -> 8.88 us
  starting transfers between devices: 0.59 us -> 25.6 us
  Pallas kernels: 0 us -> 24 us
  between operations: 14.6 us -> 0.8 us
  other arithmetic: 11.8 us -> 0.01 us
    psum x5 -> x0, waiting for transfers between devices: 519 us -> none  [the longest x3 297 us: weigh(): total = lax.psum(partial_points, 'sens')]
    psum x4 -> x0, blocking collectives: 141 us -> none  [the longest x2 62.1 us: squares(): return lax.psum(jnp.sum(residual * residual, axis=(1, 2)), 'sens')]
    dot_general x24 -> x0, matrix products: 88.3 us -> none  [the longest x3 14.4 us: adjoint_local(): jnp.einsum('cbsf,cspf->bpf', swapped, tiles, preferred_element_type=jnp.f...]
    all_to_all x0 -> x2, blocking collectives: none -> 36.5 us  [on_device(): got = lax.all_to_all(sent, 'z', 0, 0)]
    all_to_all x0 -> x4, waiting for transfers between devices: none -> 35.9 us  [the longest x2 20.1 us: on_device(): got = lax.all_to_all(sent, SENS, 0, 0)]
    pallas_call x0 -> x11, Pallas kernels: none -> 24 us  [call(): pl.pallas_call(kernel, in_specs=specs, out_specs=[VMEM] * len(outs), out_...]
    unnamed x20 -> x22, local copies, waits for them, and re-layouts: 27.2 us -> 7.1 us
    all_to_all x0 -> x4, starting transfers between devices: none -> 18.2 us  [the longest x2 11.1 us: on_device(): got = lax.all_to_all(sent, SENS, 0, 0)]
  transfers between devices with their start and end apart: 5 -> 7, of which waited for: 5 -> 7; matrix products, arithmetic and copies ran while one was open for 1% -> 0% of each run, Pallas kernels for 0% -> 1%
where the time goes in v1:
time: 135 us; the launch traced here: 134 us
  waiting for transfers between devices  38.7 us (29%)
  blocking collectives  36.5 us (27%)
  starting transfers between devices  25.6 us (19%)
  Pallas kernels  24 us (18%)
  local copies, waits for them, and re-layouts  8.88 us (7%)
    all_to_all x2, blocking collectives, on_device(): got = lax.all_to_all(sent, 'z', 0, 0)  36.5 us
    pallas_call x11, Pallas kernels, call(): pl.pallas_call(kernel, in_specs=specs, out_specs=[VMEM] * len(outs), out_...  24 us
    all_to_all x2, waiting for transfers between devices, on_device(): got = lax.all_to_all(sent, SENS, 0, 0)  20.1 us
    all_to_all x2, starting transfers between devices, on_device(): got = lax.all_to_all(sent, SENS, 0, 0)  11.1 us
    all_to_all x1, waiting for transfers between devices, on_device(): weighted_0 = lax.all_to_all(sent, SENS, 0, 0)  8.23 us
    all_to_all x1, waiting for transfers between devices, on_device(): weighted_1 = lax.all_to_all(sent, SENS, 0, 0)  7.54 us
    ppermute x3, starting transfers between devices, swap(): return lax.ppermute(block, 'core', [(0, 1), (1, 0)])  7.31 us
    unnamed x22, local copies, waits for them, and re-layouts  7.1 us
  transfers between devices with their start and end apart: 7, of which 7 were waited for; matrix products, arithmetic and copies ran while one was open for 0% of the time, Pallas kernels for 1%

profile of v1, /device:TPU:1, one launch (start us, length us, event | category | flops | bytes accessed | tf_op | source)
XLA Modules:
  0.0 134.4 jit_solution(1427182774368586292)
XLA Ops:
  0.6 0.0 copy-start.8
  0.6 0.7 broadcast_in_dim.2
  1.3 0.1 reshape.21.noise
  1.4 1.0 pad.4
  2.4 0.0 copy-start
  2.4 2.1 %copy-done = bf16[2,40,64,384]{3,2,1,0:T(8,128)(2,1)S(1)} copy-done((bf16[2,40,64,384]{3,2,1,0:T(8,128)(2,1)S(1)}, bf16[2,40,64,384]{3,2,1,0:T(8,128)(2,1)}, u32[]{:S(2)}) %copy-start) | copy-done | bytes 3932184
  4.5 0.0 copy-start.3
  4.5 1.1 copy-done.3
  5.6 0.0 copy-start.5
  5.6 1.1 copy-done.5
  6.7 0.0 copy-start.9
  6.7 0.7 copy-done.9
  7.4 0.0 copy-start.4
  7.4 0.0 copy-start.6
  7.4 0.0 copy-start.10
  7.4 6.3 %first.1 = bf16[16,112,128]{2,1,0:T(8,128)(2,1)} custom-call(f32[160,384]{1,0:T(8,128)S(1)} %bitcast.3, f32[160,1]{1,0:T(8,128)S(1)} %reshape.21.noise, bf16[2,40,64,384]{3,2,1,0:T(8,128)(2,1)S(1)} %copy-done, bf16[384,768]{1,0:T(8,128)(2,1)S(1)} %copy-done.5, bf16[384,768]{1,0:T(8,128)(2,1)S(1)} %copy-done.3, f32[8,768]{1,0:T(8,128)S(1)} %copy-done.9), custom_call_target="tpu_custom_call" | custom-call | tf_op jit(solution)/shard_map/first/pallas_call | solution.py:384
  13.7 7.6 %all-to-all-start = ((bf16[16,112,128]{2,1,0:T(8,128)(2,1)}), bf16[16,112,128]{2,1,0:T(8,128)(2,1)S(1)}, u32[]{:S(2)}, u32[]{:S(2)}) async-start(bf16[16,112,128]{2,1,0:T(8,128)(2,1)} %first.1), calls=%async_computation | async-start | bytes 917504 | tf_op jit(solution)/shard_map/all_to_all | solution.py:429
  21.3 0.0 copy-done.8
  21.4 9.9 %all-to-all-done.got = bf16[16,112,128]{2,1,0:T(8,128)(2,1)S(1)} async-done(((bf16[16,112,128]{2,1,0:T(8,128)(2,1)}), bf16[16,112,128]{2,1,0:T(8,128)(2,1)S(1)}, u32[]{:S(2)}, u32[]{:S(2)}) %all-to-all-start) | async-done | bytes 458784 | tf_op jit(solution)/shard_map/all_to_all | solution.py:429
  31.3 0.8 weigh.1
  32.1 3.6 %all-to-all-start.1 = ((bf16[16,96,128]{2,1,0:T(8,128)(2,1)}), bf16[16,96,128]{2,1,0:T(8,128)(2,1)S(1)}, u32[]{:S(2)}, u32[]{:S(2)}) async-start(bf16[16,96,128]{2,1,0:T(8,128)(2,1)} %get-tuple-element.12), calls=%async_computation.1 | async-start | bytes 786432 | tf_op jit(solution)/shard_map/all_to_all | solution.py:438
  35.6 8.2 %all-to-all-done.1.weighted = bf16[16,96,128]{2,1,0:T(8,128)(2,1)S(1)} async-done(((bf16[16,96,128]{2,1,0:T(8,128)(2,1)}), bf16[16,96,128]{2,1,0:T(8,128)(2,1)S(1)}, u32[]{:S(2)}, u32[]{:S(2)}) %all-to-all-start.1) | async-done | bytes 393248 | tf_op jit(solution)/shard_map/all_to_all | solution.py:438
  43.9 0.0 copy-done.4
  43.9 0.0 copy-done.6
  43.9 0.0 copy-done.10
  43.9 0.0 copy-start.1
  43.9 2.1 %copy-done.1 = bf16[2,40,64,384]{3,2,1,0:T(8,128)(2,1)S(1)} copy-done((bf16[2,40,64,384]{3,2,1,0:T(8,128)(2,1)S(1)}, bf16[2,40,64,384]{3,2,1,0:T(8,128)(2,1)}, u32[]{:S(2)}) %copy-start.1) | copy-done | bytes 3932184
  46.0 5.9 %forward.1 = (f32[80,384]{1,0:T(8,128)S(1)}, f32[80,384]{1,0:T(8,128)S(1)}) custom-call(s32[1]{0:T(128)} %bitcast.1.core, bf16[16,96,128]{2,1,0:T(8,128)(2,1)S(1)} %all-to-all-done.1.weighted, f32[64,384]{1,0:T(8,128)S(1)} %copy-done.8, bf16[2,40,64,384]{3,2,1,0:T(8,128)(2,1)S(1)} %copy-done.1, bf16[384,768]{1,0:T(8,128)(2,1)S(1)} %copy-done.6, ...), custom_call_target="tpu_custom_call" | custom-call | tf_op jit(solution)/shard_map/forward/pallas_call | solution.py:384
  51.9 3.0 %collective-permute-start = (f32[80,384]{1,0:T(8,128)S(1)}, f32[80,384]{1,0:T(8,128)S(1)}, u32[]{:S(2)}, u32[]{:S(2)}) collective-permute-start(f32[80,384]{1,0:T(8,128)S(1)} %get-tuple-element.14), channel_id=1, source_target_pairs={{0,1},{1,0},{2,3},{3,2},{4,5},{5,4},{6,7},{7,6},{8,9},{9,8},{10,11... | collective-permute-start | bytes 368648 | tf_op jit(solution)/shard_map/ppermute | solution.py:419
  54.9 1.0 collective-permute-done.got
  56.0 24.0 %all_to_all.30.got = bf16[8,80,384]{2,1,0:T(8,128)(2,1)S(1)} all-to-all(bf16[8,80,384]{2,1,0:T(8,128)(2,1)S(1)} %spread.1), channel_id=1, replica_groups=mesh['y'=4,'x'=4,'z'=8,'core'=2] {'z'}, dimensions={0} | all-to-all | bytes 983040 | tf_op jit(solution)/shard_map/all_to_all | solution.py:455
  79.9 0.1 gather.1.mine
  80.0 1.8 %collective-permute-start.1 = (f32[80,384]{1,0:T(8,128)S(1)}, f32[80,384]{1,0:T(8,128)S(1)}, u32[]{:S(2)}, u32[]{:S(2)}) collective-permute-start(f32[80,384]{1,0:T(8,128)S(1)} %gather.1.mine), channel_id=1, source_target_pairs={{0,1},{1,0},{2,3},{3,2},{4,5},{5,4},{6,7},{7,6},{8,9},{9,8},{10,11... | collective-permute-start | bytes 368648 | tf_op jit(solution)/shard_map/ppermute | solution.py:419
  81.8 1.0 collective-permute-done.1.theirs
  82.8 0.0 copy-done.2
  82.8 6.6 %second.1 = (bf16[16,112,128]{2,1,0:T(8,128)(2,1)}, f32[160,384]{1,0:T(8,128)S(1)}, f32[8,128]{1,0:T(8,128)S(1)}) custom-call(s32[1]{0:T(128)} %bitcast.1.core, f32[80,384]{1,0:T(8,128)S(1)} %gather.1.mine, f32[80,384]{1,0:T(8,128)S(1)} %collective-permute-done.1.theirs, f32[160,384]{1,0:T(8,128)S(1)} %bitcast.4, f32[160,1]{1,0:T(8,128)S(1)} %reshape.21.noise, ...), custom_call_target="tpu_custom_call" | custom-call | tf_op jit(solution)/shard_map/second/pallas_call | solution.py:384
  89.5 3.6 %all-to-all-start.3 = ((bf16[16,112,128]{2,1,0:T(8,128)(2,1)}), bf16[16,112,128]{2,1,0:T(8,128)(2,1)S(1)}, u32[]{:S(2)}, u32[]{:S(2)}) async-start(bf16[16,112,128]{2,1,0:T(8,128)(2,1)} %get-tuple-element.16), calls=%async_computation.3 | async-start | bytes 917504 | tf_op jit(solution)/shard_map/all_to_all | solution.py:466
  93.0 10.2 %all-to-all-done.3.got = bf16[16,112,128]{2,1,0:T(8,128)(2,1)S(1)} async-done(((bf16[16,112,128]{2,1,0:T(8,128)(2,1)}), bf16[16,112,128]{2,1,0:T(8,128)(2,1)S(1)}, u32[]{:S(2)}, u32[]{:S(2)}) %all-to-all-start.3) | async-done | bytes 458784 | tf_op jit(solution)/shard_map/all_to_all | solution.py:466
  103.3 0.9 weigh_next.1
  104.2 3.6 %all-to-all-start.4 = ((bf16[16,96,128]{2,1,0:T(8,128)(2,1)}), bf16[16,96,128]{2,1,0:T(8,128)(2,1)S(1)}, u32[]{:S(2)}, u32[]{:S(2)}) async-start(bf16[16,96,128]{2,1,0:T(8,128)(2,1)} %get-tuple-element.18), calls=%async_computation.4 | async-start | bytes 786432 | tf_op jit(solution)/shard_map/all_to_all | solution.py:475
  107.8 0.0 copy-done.7
  107.8 1.1 site_0.1
  108.9 7.5 %all-to-all-done.4.weighted = bf16[16,96,128]{2,1,0:T(8,128)(2,1)S(1)} async-done(((bf16[16,96,128]{2,1,0:T(8,128)(2,1)}), bf16[16,96,128]{2,1,0:T(8,128)(2,1)S(1)}, u32[]{:S(2)}, u32[]{:S(2)}) %all-to-all-start.4) | async-done | bytes 393248 | tf_op jit(solution)/shard_map/all_to_all | solution.py:475
  116.4 1.1 site_1.1
  117.5 2.5 %collective-permute-start.2 = (f32[32,384]{1,0:T(8,128)S(1)}, f32[32,384]{1,0:T(8,128)S(1)}, u32[]{:S(2)}, u32[]{:S(2)}) collective-permute-start(f32[32,384]{1,0:T(8,128)S(1)} %pad_maximum_fusion.mine), channel_id=1, source_target_pairs={{0,1},{1,0},{2,3},{3,2},{4,5},{5,4},{6,7},{7,6},{8,9},{9,8},{10,11... | collective-permute-start | bytes 147464 | tf_op jit(solution)/shard_map/ppermute | solution.py:419
  120.0 0.9 collective-permute-done.2.got
  120.9 12.5 %all_to_all.31.got = bf16[8,32,384]{2,1,0:T(8,128)(2,1)S(1)} all-to-all(bf16[8,32,384]{2,1,0:T(8,128)(2,1)S(1)} %spread_sites.1), channel_id=1, replica_groups=mesh['y'=4,'x'=4,'z'=8,'core'=2] {'z'}, dimensions={0} | all-to-all | bytes 393216 | tf_op jit(solution)/shard_map/all_to_all | solution.py:496
  133.4 1.0 last.1
  (6 shorter events, 0.1 us)
Async XLA Ops:
  0.6 20.7 %copy-start.8 = (f32[64,384]{1,0:T(8,128)S(1)}, f32[64,384]{1,0:T(8,128)}, u32[]{:S(2)}) copy-start(f32[64,384]{1,0:T(8,128)} %prior.5) | copy-start | bytes 294916
  2.4 2.1 %copy-start = (bf16[2,40,64,384]{3,2,1,0:T(8,128)(2,1)S(1)}, bf16[2,40,64,384]{3,2,1,0:T(8,128)(2,1)}, u32[]{:S(2)}) copy-start(bf16[2,40,64,384]{3,2,1,0:T(8,128)(2,1)} %tiles.8) | copy-start | bytes 11796484
  4.5 1.1 copy-start.3
  5.6 1.1 copy-start.5
  6.7 0.7 copy-start.9
  7.4 36.5 %copy-start.4 = (bf16[384,768]{1,0:T(8,128)(2,1)S(1)}, bf16[384,768]{1,0:T(8,128)(2,1)}, u32[]{:S(2)}) copy-start(bf16[384,768]{1,0:T(8,128)(2,1)} %constant.48.clone.low) | copy-start | bytes 1769476
  7.4 36.5 %copy-start.6 = (bf16[384,768]{1,0:T(8,128)(2,1)S(1)}, bf16[384,768]{1,0:T(8,128)(2,1)}, u32[]{:S(2)}) copy-start(bf16[384,768]{1,0:T(8,128)(2,1)} %constant.47.clone.high) | copy-start | bytes 1769476
  7.4 36.5 %copy-start.10 = (f32[8,768]{1,0:T(8,128)S(1)}, f32[8,768]{1,0:T(8,128)}, u32[]{:S(2)}) copy-start(f32[8,768]{1,0:T(8,128)} %constant.49.clone.weights) | copy-start | bytes 73732
  13.7 17.5 %all-to-all-start = ((bf16[16,112,128]{2,1,0:T(8,128)(2,1)}), bf16[16,112,128]{2,1,0:T(8,128)(2,1)S(1)}, u32[]{:S(2)}, u32[]{:S(2)}) async-start(bf16[16,112,128]{2,1,0:T(8,128)(2,1)} %first.1), calls=%async_computation | async-start | bytes 917504 | tf_op jit(solution)/shard_map/all_to_all | solution.py:429
  32.1 11.8 %all-to-all-start.1 = ((bf16[16,96,128]{2,1,0:T(8,128)(2,1)}), bf16[16,96,128]{2,1,0:T(8,128)(2,1)S(1)}, u32[]{:S(2)}, u32[]{:S(2)}) async-start(bf16[16,96,128]{2,1,0:T(8,128)(2,1)} %get-tuple-element.12), calls=%async_computation.1 | async-start | bytes 786432 | tf_op jit(solution)/shard_map/all_to_all | solution.py:438
  43.9 2.1 %copy-start.1 = (bf16[2,40,64,384]{3,2,1,0:T(8,128)(2,1)S(1)}, bf16[2,40,64,384]{3,2,1,0:T(8,128)(2,1)}, u32[]{:S(2)}) copy-start(bf16[2,40,64,384]{3,2,1,0:T(8,128)(2,1)} %tiles.8) | copy-start | bytes 11796484
  46.0 36.8 %copy-start.2 = (bf16[2,40,64,384]{3,2,1,0:T(8,128)(2,1)S(1)}, bf16[2,40,64,384]{3,2,1,0:T(8,128)(2,1)}, u32[]{:S(2)}) copy-start(bf16[2,40,64,384]{3,2,1,0:T(8,128)(2,1)} %tiles.8) | copy-start | bytes 11796484
  51.9 4.0 %collective-permute-start = (f32[80,384]{1,0:T(8,128)S(1)}, f32[80,384]{1,0:T(8,128)S(1)}, u32[]{:S(2)}, u32[]{:S(2)}) collective-permute-start(f32[80,384]{1,0:T(8,128)S(1)} %get-tuple-element.14), channel_id=1, source_target_pairs={{0,1},{1,0},{2,3},{3,2},{4,5},{5,4},{6,7},{7,6},{8,9},{9,8},{10,11... | collective-permute-start | bytes 368648 | tf_op jit(solution)/shard_map/ppermute | solution.py:419
  80.0 2.8 %collective-permute-start.1 = (f32[80,384]{1,0:T(8,128)S(1)}, f32[80,384]{1,0:T(8,128)S(1)}, u32[]{:S(2)}, u32[]{:S(2)}) collective-permute-start(f32[80,384]{1,0:T(8,128)S(1)} %gather.1.mine), channel_id=1, source_target_pairs={{0,1},{1,0},{2,3},{3,2},{4,5},{5,4},{6,7},{7,6},{8,9},{9,8},{10,11... | collective-permute-start | bytes 368648 | tf_op jit(solution)/shard_map/ppermute | solution.py:419
  82.8 24.9 %copy-start.7 = (bf16[2,4,64,384]{3,2,1,0:T(8,128)(2,1)S(1)}, bf16[2,4,64,384]{3,2,1,0:T(8,128)(2,1)}, u32[]{:S(2)}) copy-start(bf16[2,4,64,384]{3,2,1,0:T(8,128)(2,1)} %tiles.9) | copy-start | bytes 1179652
  89.5 13.8 %all-to-all-start.3 = ((bf16[16,112,128]{2,1,0:T(8,128)(2,1)}), bf16[16,112,128]{2,1,0:T(8,128)(2,1)S(1)}, u32[]{:S(2)}, u32[]{:S(2)}) async-start(bf16[16,112,128]{2,1,0:T(8,128)(2,1)} %get-tuple-element.16), calls=%async_computation.3 | async-start | bytes 917504 | tf_op jit(solution)/shard_map/all_to_all | solution.py:466
  104.2 12.2 %all-to-all-start.4 = ((bf16[16,96,128]{2,1,0:T(8,128)(2,1)}), bf16[16,96,128]{2,1,0:T(8,128)(2,1)S(1)}, u32[]{:S(2)}, u32[]{:S(2)}) async-start(bf16[16,96,128]{2,1,0:T(8,128)(2,1)} %get-tuple-element.18), calls=%async_computation.4 | async-start | bytes 786432 | tf_op jit(solution)/shard_map/all_to_all | solution.py:475
  117.5 3.3 %collective-permute-start.2 = (f32[32,384]{1,0:T(8,128)S(1)}, f32[32,384]{1,0:T(8,128)S(1)}, u32[]{:S(2)}, u32[]{:S(2)}) collective-permute-start(f32[32,384]{1,0:T(8,128)S(1)} %pad_maximum_fusion.mine), channel_id=1, source_target_pairs={{0,1},{1,0},{2,3},{3,2},{4,5},{5,4},{6,7},{7,6},{8,9},{9,8},{10,11... | collective-permute-start | bytes 147464 | tf_op jit(solution)/shard_map/ppermute | solution.py:419

commit v2 on v1

--- a/solution.py
+++ b/solution.py
@@ -18,6 +18,7 @@
 F32 = jnp.float32
 BF16 = jnp.bfloat16
 VMEM = pl.BlockSpec(memory_space=pltpu.VMEM)
+HBM = pl.BlockSpec(memory_space=pltpu.HBM)
 SMEM = pl.BlockSpec(memory_space=pltpu.SMEM)
 
 
@@ -28,9 +29,14 @@
     both = np.concatenate([np.cos(angle), -np.sin(angle)], axis=1)
     high = both.astype(BF16)
     low = (both - high.astype(np.float64)).astype(BF16)
-    weights = np.where((steps == 0) | (steps == freqs - 1), 1.0, 2.0) / padded
-    weights = np.tile(weights[None], (8, 2)).astype(np.float32)
-    return jnp.asarray(high), jnp.asarray(low), jnp.asarray(weights)
+    return jnp.asarray(high), jnp.asarray(low)
+
+
+def frequency_weights(freqs):
+    at = lax.broadcasted_iota(jnp.int32, (1, 2 * freqs), 1)
+    at = jnp.where(at < freqs, at, at - freqs)
+    padded = 2 * (freqs - 1)
+    return jnp.where((at == 0) | (at == freqs - 1), 1.0 / padded, 2.0 / padded)
 
 
 def product(left, high, low):
@@ -74,57 +80,107 @@
     return jnp.sum(total, axis=1, keepdims=True)
 
 
-def send_points(series, tiles, high, low, weights, spec, out):
+def bands_of(source, target, done, first=0):
+    def copy(band):
+        at = pl.ds(pl.multiple_of(band * 16, 16), 16)
+        return pltpu.make_async_copy(
+            source.at[:, :, at, :], target.at[:, :, at, :], done.at[first + band]
+        )
+
+    return copy
+
+
+def groups_of(source, target, done):
+    def copy(group):
+        at = pl.ds(group * 8, 8)
+        return pltpu.make_async_copy(source.at[:, at], target.at[:, at], done.at[group])
+
+    return copy
+
+
+def send_points(series, tiles, copy, high, low, spec, out):
     sens, points, freqs = tiles.shape[1:]
-    spec[...] = product(series[...], high[...], low[...]) * weights[0:1, :]
+    pair = product(series[...], high[...], low[...]) * frequency_weights(freqs)
+    spec[:, : 2 * freqs] = pair
+    spec[:, 2 * freqs :] = pair[:, :freqs] + pair[:, freqs:]
     blocks = freqs // LANES
+    step = 16
 
     def part(index, _):
         band = index // blocks
         block = index % blocks
-        lanes = pl.ds(pl.multiple_of(block * LANES, LANES), LANES)
-        sines = pl.ds(pl.multiple_of(freqs + block * LANES, LANES), LANES)
-        range_ = pl.ds(pl.multiple_of(band * BAND, BAND), BAND)
+        lanes = [
+            pl.ds(pl.multiple_of(c * freqs + block * LANES, LANES), LANES) for c in range(3)
+        ]
+        range_ = pl.ds(pl.multiple_of(band * step, step), step)
+
+        @pl.when(block == 0)
+        def _():
+            copy(band).wait()
 
         def group(g, acc):
             acc = list(acc)
             rows = [pl.ds(pl.multiple_of(b * sens + g * 8, 8), 8) for b in range(REALS)]
-            real = [spec[r, lanes] for r in rows]
-            imag = [spec[r, sines] for r in rows]
+            values = [[spec[r, c] for c in lanes] for r in rows]
             for j in range(8):
-                tr = tiles[0, g * 8 + j, range_, lanes].astype(F32)
-                ti = tiles[1, g * 8 + j, range_, lanes].astype(F32)
+                tr = tiles[0, g * 8 + j, range_, lanes[0]].astype(F32)
+                ti = tiles[1, g * 8 + j, range_, lanes[0]].astype(F32)
+                terms = (tr, ti, tr - ti)
                 for b in range(REALS):
-                    sr = real[b][j : j + 1]
-                    si = imag[b][j : j + 1]
-                    re, im = acc[b]
-                    acc[b] = (re + (sr * tr + si * ti), im + (si * tr - sr * ti))
+                    acc[b] = tuple(
+                        acc[b][c] + values[b][c][j : j + 1] * terms[c] for c in range(3)
+                    )
             return tuple(acc)
 
-        zero = jnp.zeros((BAND, LANES), F32)
-        acc = lax.fori_loop(0, sens // 8, group, ((zero, zero),) * REALS)
+        zero = jnp.zeros((step, LANES), F32)
+        acc = lax.fori_loop(0, sens // 8, group, ((zero, zero, zero),) * REALS)
+        per = BAND // step
         parts = points // BAND
-        rows = pl.ds(pl.multiple_of(block * BAND, BAND), BAND)
+        at = pl.ds(pl.multiple_of(block * BAND + (band % per) * step, step), step)
         for b in range(REALS):
-            for c in range(2):
-                out[(c * REALS + b) * parts + band, rows, :] = acc[b][c].astype(BF16)
+            first, second, third = acc[b]
+            out[b * parts + band // per, at, :] = (first + second).astype(BF16)
+            out[(REALS + b) * parts + band // per, at, :] = (third - first + second).astype(BF16)
         return 0
 
-    lax.fori_loop(0, (points // BAND) * blocks, part, 0)
-
-
-def first_kernel(series, noise, tiles, high, low, weights, out, spec, *, sens):
-    values = series[...]
-    noisy = values * noise[...]
-    columns = [band_sum(values, values, b * sens, sens) for b in range(REALS)]
-    columns += [band_sum(values, noisy, b * sens, sens) for b in range(REALS)]
-    write_scalars(out, columns)
-    send_points(series, tiles, high, low, weights, spec, out)
+    lax.fori_loop(0, (points // step) * blocks, part, 0)
+
+
+def first_kernel(
+    records, noise, tiles_in, high_in, low_in, out, series, column, raw, raw_noise, tiles, high, low, spec, done
+):
+    reals, sens, steps = records.shape
+    moves = ((records, raw), (noise, raw_noise), (high_in, high), (low_in, low))
+    copies = [pltpu.make_async_copy(*move, done.at[k]) for k, move in enumerate(moves)]
+    fetch = bands_of(tiles_in, tiles, done, len(copies))
+    for copy in copies + [fetch(k) for k in range(tiles.shape[2] // 16)]:
+        copy.start()
+    copies[0].wait()
+    copies[1].wait()
+    row = lax.broadcasted_iota(jnp.int32, (sens, sens), 0)
+    noises = jnp.where(row == lane_of((sens, sens)), raw_noise[...], 0.0)
+    noises = jnp.sum(noises, axis=1, keepdims=True)
+    column[...] = noises
+    series[...] = jnp.zeros_like(series)
+    columns = [[], []]
+    for b in range(reals):
+        series[b * sens : (b + 1) * sens, :steps] = raw[b]
+    for b in range(reals):
+        values = series[b * sens : (b + 1) * sens, :]
+        columns[0].append(band_sum(values, values, 0, sens))
+        columns[1].append(band_sum(values, values * noises, 0, sens))
+    write_scalars(out, columns[0] + columns[1])
+    copies[2].wait()
+    copies[3].wait()
+    send_points(series, tiles, fetch, high, low, spec, out)
 
 
 def second_kernel(
-    core, mine, theirs, series, noise, begin, tiles, high, low, weights, out, residual, alpha, image, spec
+    core, mine, theirs, series, noise, begin, tiles_in, high, low, out, residual, alpha, image, tiles, spec, done
 ):
+    fetch = bands_of(tiles_in, tiles, done)
+    for k in range(tiles.shape[2] // 16):
+        fetch(k).start()
     half, freqs = mine.shape
     sens = 2 * half // REALS
     image[pl.ds(pl.multiple_of(core[0] * half, 8), half), :] = mine[...]
@@ -140,7 +196,7 @@
         tile = jnp.where(lane == b, scale, tile)
         rows = slice(b * sens, (b + 1) * sens)
         values = series[rows, :]
-        noisy = noise[rows, :]
+        noisy = noise[...]
         left = values - scale * (jnp.where(real, image[rows, :], 0.0) + noisy * values)
         residual[rows, :] = left
         columns[0].append(band_sum(left, left, 0, sens))
@@ -148,7 +204,7 @@
         columns[2].append(band_sum(left, values * noisy, 0, sens))
     alpha[...] = tile
     write_scalars(out, columns[0] + columns[1] + columns[2])
-    send_points(residual, tiles, high, low, weights, spec, out)
+    send_points(residual, tiles, fetch, high, low, spec, out)
 
 
 def sum_message(got):
@@ -197,13 +253,14 @@
                 lanes = slice(block * LANES, (block + 1) * LANES)
                 inverse = 1.0 / prior[h * BAND + row : h * BAND + row + 16, lanes]
                 for b in range(REALS):
-                    for c in range(2):
-                        k = (c * REALS + b) * parts + h
-                        at = slice(block * BAND + row, block * BAND + row + 16)
-                        part = weighted[k, at, :].astype(F32)
-                        wide[k, at, :] = part
-                        term = part * part * inverse
-                        energy[b] = energy[b] + (term[:8] + term[8:])
+                    at = slice(block * BAND + row, block * BAND + row + 16)
+                    re = weighted[b * parts + h, at, :].astype(F32)
+                    im = weighted[(REALS + b) * parts + h, at, :].astype(F32)
+                    wide[b * parts + h, at, :] = re
+                    wide[(REALS + b) * parts + h, at, :] = im
+                    wide[(2 * REALS + b) * parts + h, at, :] = re + im
+                    term = (re * re + im * im) * inverse
+                    energy[b] = energy[b] + (term[:8] + term[8:])
     return [
         jnp.sum(jnp.sum(e, axis=0, keepdims=True), axis=1, keepdims=True) for e in energy
     ]
@@ -221,30 +278,28 @@
 
 def site_sums(tiles, wide, sites, reals, block, lanes):
     sums = {}
+    parts = tiles.shape[2] // BAND
     for p in range(0, tiles.shape[2], 16):
         h, row = divmod(p, BAND)
-        pair = [[tiles[c, s, pl.ds(p, 16), lanes].astype(F32) for c in range(2)] for s in sites]
+        terms = []
+        for s in sites:
+            tr, ti = (tiles[c, s, pl.ds(p, 16), lanes].astype(F32) for c in range(2))
+            terms.append((tr, ti, tr + ti))
         for q in (0, 8):
+            at = pl.ds(pl.multiple_of(block * BAND + row + q, 8), 8)
             for b in reals:
-                at = pl.ds(pl.multiple_of(block * BAND + row + q, 8), 8)
-                parts = tiles.shape[2] // BAND
-                wr = wide[b * parts + h, at, :]
-                wi = wide[(REALS + b) * parts + h, at, :]
+                values = [wide[(c * REALS + b) * parts + h, at, :] for c in range(3)]
                 for j in range(len(sites)):
-                    tr = pair[j][0][q : q + 8]
-                    ti = pair[j][1][q : q + 8]
-                    re = wr * tr - wi * ti
-                    im = wr * ti + wi * tr
+                    new = [values[c] * terms[j][c][q : q + 8] for c in range(3)]
                     if (j, b) in sums:
-                        re = sums[j, b][0] + re
-                        im = sums[j, b][1] + im
-                    sums[j, b] = (re, im)
-    return sums
-
-
-def synthesize(rows, weights, high, low, energy, stride):
+                        new = [x + y for x, y in zip(sums[j, b], new)]
+                    sums[j, b] = new
+    return {k: (x - y, z - x - y) for k, (x, y, z) in sums.items()}
+
+
+def synthesize(rows, high, low, energy, stride):
     count, freqs = rows.shape[0], rows.shape[1] // 2
-    scaled = rows[...] * weights[0:1, :]
+    scaled = rows[...] * frequency_weights(freqs)
     series = product(scaled[:, :freqs], high[:, :freqs], low[:, :freqs]) + product(
         scaled[:, freqs:], high[:, freqs:], low[:, freqs:]
     )
@@ -258,8 +313,13 @@
     return jnp.where(lane == freqs - 1, carried, series)
 
 
-def forward_kernel(core, weighted, prior, tiles, high, low, weights, mine, other, wide, rows, full):
+def forward_kernel(
+    core, weighted, prior, tiles_in, high, low, mine, other, wide, rows, full, tiles, done
+):
     sens, points, freqs = tiles.shape[1:]
+    fetch = groups_of(tiles_in, tiles, done)
+    for k in range(sens // 8):
+        fetch(k).start()
     energy = widen(weighted, prior, wide)
     place = lax.broadcasted_iota(jnp.int32, (8, LANES), 0)
     blocks = freqs // LANES
@@ -269,6 +329,10 @@
         block = index % blocks
         lanes = pl.ds(pl.multiple_of(block * LANES, LANES), LANES)
         sines = pl.ds(pl.multiple_of(freqs + block * LANES, LANES), LANES)
+
+        @pl.when(block == 0)
+        def _():
+            fetch(g).wait()
 
         def pair(k):
             sums = site_sums(tiles, wide, [g * 8 + k, g * 8 + k + 4], range(REALS), block, lanes)
@@ -295,7 +359,7 @@
 
     lax.fori_loop(0, (sens // 8) * blocks, part, 0)
     half = REALS * sens // 2
-    series = synthesize(rows, weights, high, low, energy + energy, 8)
+    series = synthesize(rows, high, low, energy + energy, 8)
     row = lax.broadcasted_iota(jnp.int32, (half, freqs), 0)
     lane = lane_of((half, freqs))
     carried = series[:half, freqs - 1 :]
@@ -305,7 +369,7 @@
     other[...] = full[pl.ds(pl.multiple_of((1 - core[0]) * half, 8), half), :]
 
 
-def site_kernel(weighted, prior, tiles, high, low, weights, out, wide, rows):
+def site_kernel(weighted, prior, tiles, high, low, out, wide, rows):
     freqs = tiles.shape[3]
     energy = widen(weighted, prior, wide)
     place = lax.broadcasted_iota(jnp.int32, (8, LANES), 0)
@@ -326,7 +390,7 @@
         return 0
 
     lax.fori_loop(0, freqs // LANES, part, 0)
-    out[...] = synthesize(rows, weights, high, low, energy, REALS)
+    out[...] = synthesize(rows, high, low, energy, REALS)
 
 
 def spread_kernel(mine, got, out, *, stride, begin):
@@ -380,14 +444,22 @@
         predicted[b] = (first * low + second * high)[:, :steps]
 
 
-def call(kernel, name, outs, scratch, specs, *args):
+def in_hbm(array):
+    return pltpu.with_memory_space_constraint(array, pltpu.HBM)
+
+
+def call(kernel, name, outs, scratch, specs, *args, semaphores=0, limit=24 * 2**20):
+    scratch = [pltpu.VMEM(*one) for one in scratch]
+    args = [in_hbm(arg) if spec is HBM else arg for arg, spec in zip(args, specs)]
+    if semaphores:
+        scratch.append(pltpu.SemaphoreType.DMA((semaphores,)))
     return pl.pallas_call(
         kernel,
         in_specs=specs,
         out_specs=[VMEM] * len(outs),
         out_shape=[jax.ShapeDtypeStruct(*out) for out in outs],
-        scratch_shapes=[pltpu.VMEM(*one) for one in scratch],
-        compiler_params=pltpu.CompilerParams(vmem_limit_bytes=24 * 2**20),
+        scratch_shapes=scratch,
+        compiler_params=pltpu.CompilerParams(vmem_limit_bytes=limit),
         name=name,
     )(*args)
 
@@ -406,25 +478,30 @@
     pick = lax.rem(place * BAND // points, reals).astype(jnp.int32).reshape(1)
     count = reals * sensors
     half = count // 2
-    series = jnp.pad(records, ((0, 0), (0, 0), (0, freqs - steps))).reshape(count, freqs)
-    noisy = jnp.broadcast_to(noise[None, :], (reals, sensors)).reshape(count, 1)
     block_rows = BAND * freqs // LANES
     message = ((senders, block_rows + EXTRA, LANES), BF16)
     weighted_shape = (senders, block_rows, LANES)
+    wide_shape = (3 * senders // 2, block_rows, LANES)
     spectra = ((count, 2 * freqs), F32)
+    sums = ((count, 3 * freqs), F32)
     rows = ((count, freqs), F32)
     tile = ((8, LANES), F32)
 
     def swap(block):
         return lax.ppermute(block, "core", [(0, 1), (1, 0)])
 
-    (sent,) = call(
-        functools.partial(first_kernel, sens=sensors),
+    bands = points // 16
+    local = (tiles.shape, BF16)
+    sent, series, noisy = call(
+        first_kernel,
         "first",
-        [message],
-        [spectra],
-        [VMEM] * 6,
-        *(series, noisy, tiles, *tables),
+        [message, rows, ((sensors, 1), F32)],
+        [(records.shape, F32), ((1, sensors), F32), local]
+        + [(table.shape, BF16) for table in tables]
+        + [sums],
+        [HBM] * 5,
+        *(records, noise.reshape(1, sensors), tiles, *tables),
+        semaphores=4 + bands,
     )
     got = lax.all_to_all(sent, SENS, 0, 0)
     sent, points_0, begin = call(
@@ -440,9 +517,10 @@
         forward_kernel,
         "forward",
         [((half, freqs), F32)] * 2,
-        [(weighted_shape, F32), spectra, rows],
-        [SMEM] + [VMEM] * 6,
+        [(wide_shape, F32), spectra, rows, local],
+        [SMEM, VMEM, VMEM, HBM, VMEM, VMEM],
         *(core, weighted_0, prior, tiles, *tables),
+        semaphores=sensors // 8,
     )
     (sent,) = call(
         functools.partial(spread_kernel, stride=8, begin=0),
@@ -459,9 +537,10 @@
         second_kernel,
         "second",
         [message, rows, tile],
-        [rows, spectra],
-        [SMEM] + [VMEM] * 9,
+        [rows, local, sums],
+        [SMEM] + [VMEM] * 5 + [HBM, VMEM, VMEM],
         *(core, mine, theirs, series, noisy, begin, tiles, *tables),
+        semaphores=bands,
     )
     got = lax.all_to_all(sent, SENS, 0, 0)
     sent, later = call(
@@ -479,8 +558,8 @@
             site_kernel,
             name,
             [((reals * sites, freqs), F32)],
-            [(weighted_shape, F32), ((reals * sites, 2 * freqs), F32)],
-            [VMEM] * 6,
+            [(wide_shape, F32), ((reals * sites, 2 * freqs), F32)],
+            [VMEM] * 5,
             *(weighted, prior, gauges, *tables),
         )[0]
 

time: 135 us -> 129 us (0.956)
  local copies, waits for them, and re-layouts: 8.88 us -> 0.03 us
  Pallas kernels: 24 us -> 27.2 us
    unnamed x22 -> x8, local copies, waits for them, and re-layouts: 7.1 us -> 0.02 us
    pallas_call x11, Pallas kernels: 24 us -> 27.2 us  [call(): pl.pallas_call(kernel, in_specs=specs, out_specs=[VMEM] * len(outs), out_...]
where the time goes in v2:
time: 129 us
  waiting for transfers between devices  38.7 us (30%)
  blocking collectives  36.5 us (28%)
  Pallas kernels  27.2 us (21%)
  starting transfers between devices  25.6 us (20%)
    all_to_all x2, blocking collectives, on_device(): got = lax.all_to_all(sent, 'z', 0, 0)  36.5 us
    pallas_call x11, Pallas kernels, call(): pl.pallas_call(kernel, in_specs=specs, out_specs=[VMEM] * len(outs), out_...  27.2 us
    all_to_all x2, waiting for transfers between devices, on_device(): got = lax.all_to_all(sent, SENS, 0, 0)  20.1 us
    all_to_all x2, starting transfers between devices, on_device(): got = lax.all_to_all(sent, SENS, 0, 0)  11.2 us
    all_to_all x1, waiting for transfers between devices, on_device(): weighted_0 = lax.all_to_all(sent, SENS, 0, 0)  8.23 us
    all_to_all x1, waiting for transfers between devices, on_device(): weighted_1 = lax.all_to_all(sent, SENS, 0, 0)  7.58 us
    ppermute x3, starting transfers between devices, swap(): return lax.ppermute(block, 'core', [(0, 1), (1, 0)])  7.32 us
    all_to_all x1, starting transfers between devices, on_device(): weighted_0 = lax.all_to_all(sent, SENS, 0, 0)  3.55 us
  transfers between devices with their start and end apart: 7, of which 7 were waited for; matrix products, arithmetic and copies ran while one was open for 0% of the time, Pallas kernels for 1%

profile of v2, /device:TPU:1, one launch (start us, length us, event | category | flops | bytes accessed | tf_op | source)
XLA Modules:
  0.0 128.9 jit_solution(1034269484364107087)
XLA Ops:
  0.6 0.0 copy-start
  0.6 0.0 copy-start.1
  0.7 0.0 copy-start.3
  0.7 8.1 %first.1 = (bf16[16,112,128]{2,1,0:T(8,128)(2,1)}, f32[160,384]{1,0:T(8,128)S(1)}, f32[40,1]{1,0:T(8,128)S(1)}) custom-call(f32[4,40,383]{2,1,0:T(8,128)} %records.1, f32[1,40]{1,0:T(1,128)} %bitcast.3, bf16[2,40,64,384]{3,2,1,0:T(8,128)(2,1)} %tiles_in.5, bf16[384,768]{1,0:T(8,128)(2,1)} %constant.43.clone.high_in.high, ...), custom_call_target="tpu_custom_call" | custom-call | tf_op jit(solution)/shard_map/first/pallas_call | solution.py:456
  8.8 7.6 %all-to-all-start = ((bf16[16,112,128]{2,1,0:T(8,128)(2,1)}), bf16[16,112,128]{2,1,0:T(8,128)(2,1)S(1)}, u32[]{:S(2)}, u32[]{:S(2)}) async-start(bf16[16,112,128]{2,1,0:T(8,128)(2,1)} %get-tuple-element.15), calls=%async_computation | async-start | bytes 917504 | tf_op jit(solution)/shard_map/all_to_all | solution.py:506
  16.4 0.0 copy-done.3
  16.4 9.9 %all-to-all-done.got = bf16[16,112,128]{2,1,0:T(8,128)(2,1)S(1)} async-done(((bf16[16,112,128]{2,1,0:T(8,128)(2,1)}), bf16[16,112,128]{2,1,0:T(8,128)(2,1)S(1)}, u32[]{:S(2)}, u32[]{:S(2)}) %all-to-all-start) | async-done | bytes 458784 | tf_op jit(solution)/shard_map/all_to_all | solution.py:506
  26.3 0.8 weigh.1
  27.1 3.6 %all-to-all-start.1 = ((bf16[16,96,128]{2,1,0:T(8,128)(2,1)}), bf16[16,96,128]{2,1,0:T(8,128)(2,1)S(1)}, u32[]{:S(2)}, u32[]{:S(2)}) async-start(bf16[16,96,128]{2,1,0:T(8,128)(2,1)} %get-tuple-element.16), calls=%async_computation.1 | async-start | bytes 786432 | tf_op jit(solution)/shard_map/all_to_all | solution.py:515
  30.7 8.2 %all-to-all-done.1.weighted = bf16[16,96,128]{2,1,0:T(8,128)(2,1)S(1)} async-done(((bf16[16,96,128]{2,1,0:T(8,128)(2,1)}), bf16[16,96,128]{2,1,0:T(8,128)(2,1)S(1)}, u32[]{:S(2)}, u32[]{:S(2)}) %all-to-all-start.1) | async-done | bytes 393248 | tf_op jit(solution)/shard_map/all_to_all | solution.py:515
  38.9 0.0 copy-done
  38.9 0.0 copy-done.1
  38.9 6.2 %forward.1 = (f32[80,384]{1,0:T(8,128)S(1)}, f32[80,384]{1,0:T(8,128)S(1)}) custom-call(s32[1]{0:T(128)} %bitcast.1.core, bf16[16,96,128]{2,1,0:T(8,128)(2,1)S(1)} %all-to-all-done.1.weighted, f32[64,384]{1,0:T(8,128)S(1)} %copy-done.3, bf16[2,40,64,384]{3,2,1,0:T(8,128)(2,1)} %tiles_in.5, bf16[384,768]{1,0:T(8,128)(2,1)S(1)} %copy-done.1, ...), custom_call_target="tpu_custom_call" | custom-call | tf_op jit(solution)/shard_map/forward/pallas_call | solution.py:456
  45.2 3.0 %collective-permute-start = (f32[80,384]{1,0:T(8,128)S(1)}, f32[80,384]{1,0:T(8,128)S(1)}, u32[]{:S(2)}, u32[]{:S(2)}) collective-permute-start(f32[80,384]{1,0:T(8,128)S(1)} %get-tuple-element.18), channel_id=1, source_target_pairs={{0,1},{1,0},{2,3},{3,2},{4,5},{5,4},{6,7},{7,6},{8,9},{9,8},{10,11... | collective-permute-start | bytes 368648 | tf_op jit(solution)/shard_map/ppermute | solution.py:491
  48.2 1.0 collective-permute-done.got
  49.2 24.0 %all_to_all.30.got = bf16[8,80,384]{2,1,0:T(8,128)(2,1)S(1)} all-to-all(bf16[8,80,384]{2,1,0:T(8,128)(2,1)S(1)} %spread.1), channel_id=1, replica_groups=mesh['y'=4,'x'=4,'z'=8,'core'=2] {'z'}, dimensions={0} | all-to-all | bytes 983040 | tf_op jit(solution)/shard_map/all_to_all | solution.py:533
  73.2 0.1 gather.1.mine
  73.3 1.8 %collective-permute-start.1 = (f32[80,384]{1,0:T(8,128)S(1)}, f32[80,384]{1,0:T(8,128)S(1)}, u32[]{:S(2)}, u32[]{:S(2)}) collective-permute-start(f32[80,384]{1,0:T(8,128)S(1)} %gather.1.mine), channel_id=1, source_target_pairs={{0,1},{1,0},{2,3},{3,2},{4,5},{5,4},{6,7},{7,6},{8,9},{9,8},{10,11... | collective-permute-start | bytes 368648 | tf_op jit(solution)/shard_map/ppermute | solution.py:491
  75.1 1.0 collective-permute-done.1.theirs
  76.1 0.0 copy-start.2
  76.1 7.9 %second.1 = (bf16[16,112,128]{2,1,0:T(8,128)(2,1)}, f32[160,384]{1,0:T(8,128)S(1)}, f32[8,128]{1,0:T(8,128)S(1)}) custom-call(s32[1]{0:T(128)} %bitcast.1.core, f32[80,384]{1,0:T(8,128)S(1)} %gather.1.mine, f32[80,384]{1,0:T(8,128)S(1)} %collective-permute-done.1.theirs, f32[160,384]{1,0:T(8,128)S(1)} %get-tuple-element.19.series, ...), custom_call_target="tpu_custom_call" | custom-call | tf_op jit(solution)/shard_map/second/pallas_call | solution.py:456
  83.9 3.6 %all-to-all-start.3 = ((bf16[16,112,128]{2,1,0:T(8,128)(2,1)}), bf16[16,112,128]{2,1,0:T(8,128)(2,1)S(1)}, u32[]{:S(2)}, u32[]{:S(2)}) async-start(bf16[16,112,128]{2,1,0:T(8,128)(2,1)} %get-tuple-element.22), calls=%async_computation.3 | async-start | bytes 917504 | tf_op jit(solution)/shard_map/all_to_all | solution.py:545
  87.6 10.2 %all-to-all-done.3.got = bf16[16,112,128]{2,1,0:T(8,128)(2,1)S(1)} async-done(((bf16[16,112,128]{2,1,0:T(8,128)(2,1)}), bf16[16,112,128]{2,1,0:T(8,128)(2,1)S(1)}, u32[]{:S(2)}, u32[]{:S(2)}) %all-to-all-start.3) | async-done | bytes 458784 | tf_op jit(solution)/shard_map/all_to_all | solution.py:545
  97.8 0.9 weigh_next.1
  98.7 3.6 %all-to-all-start.4 = ((bf16[16,96,128]{2,1,0:T(8,128)(2,1)}), bf16[16,96,128]{2,1,0:T(8,128)(2,1)S(1)}, u32[]{:S(2)}, u32[]{:S(2)}) async-start(bf16[16,96,128]{2,1,0:T(8,128)(2,1)} %get-tuple-element.24), calls=%async_computation.4 | async-start | bytes 786432 | tf_op jit(solution)/shard_map/all_to_all | solution.py:554
  102.3 0.0 copy-done.2
  102.3 1.0 site_0.1
  103.3 7.6 %all-to-all-done.4.weighted = bf16[16,96,128]{2,1,0:T(8,128)(2,1)S(1)} async-done(((bf16[16,96,128]{2,1,0:T(8,128)(2,1)}), bf16[16,96,128]{2,1,0:T(8,128)(2,1)S(1)}, u32[]{:S(2)}, u32[]{:S(2)}) %all-to-all-start.4) | async-done | bytes 393248 | tf_op jit(solution)/shard_map/all_to_all | solution.py:554
  110.9 1.0 site_1.1
  111.9 2.5 %collective-permute-start.2 = (f32[32,384]{1,0:T(8,128)S(1)}, f32[32,384]{1,0:T(8,128)S(1)}, u32[]{:S(2)}, u32[]{:S(2)}) collective-permute-start(f32[32,384]{1,0:T(8,128)S(1)} %pad_maximum_fusion.mine), channel_id=1, source_target_pairs={{0,1},{1,0},{2,3},{3,2},{4,5},{5,4},{6,7},{7,6},{8,9},{9,8},{10,11... | collective-permute-start | bytes 147464 | tf_op jit(solution)/shard_map/ppermute | solution.py:491
  114.4 0.9 collective-permute-done.2.got
  115.3 12.5 %all_to_all.31.got = bf16[8,32,384]{2,1,0:T(8,128)(2,1)S(1)} all-to-all(bf16[8,32,384]{2,1,0:T(8,128)(2,1)S(1)} %spread_sites.1), channel_id=1, replica_groups=mesh['y'=4,'x'=4,'z'=8,'core'=2] {'z'}, dimensions={0} | all-to-all | bytes 393216 | tf_op jit(solution)/shard_map/all_to_all | solution.py:575
  127.8 1.0 last.1
  (4 shorter events, 0.1 us)
Async XLA Ops:
  0.6 38.3 %copy-start = (bf16[384,768]{1,0:T(8,128)(2,1)S(1)}, bf16[384,768]{1,0:T(8,128)(2,1)}, u32[]{:S(2)}) copy-start(bf16[384,768]{1,0:T(8,128)(2,1)} %constant.44.clone.low_in.low) | copy-start | bytes 1769476
  0.6 38.3 %copy-start.1 = (bf16[384,768]{1,0:T(8,128)(2,1)S(1)}, bf16[384,768]{1,0:T(8,128)(2,1)}, u32[]{:S(2)}) copy-start(bf16[384,768]{1,0:T(8,128)(2,1)} %constant.43.clone.high_in.high) | copy-start | bytes 1769476
  0.7 15.7 %copy-start.3 = (f32[64,384]{1,0:T(8,128)S(1)}, f32[64,384]{1,0:T(8,128)}, u32[]{:S(2)}) copy-start(f32[64,384]{1,0:T(8,128)} %prior.5) | copy-start | bytes 294916
  8.8 17.5 %all-to-all-start = ((bf16[16,112,128]{2,1,0:T(8,128)(2,1)}), bf16[16,112,128]{2,1,0:T(8,128)(2,1)S(1)}, u32[]{:S(2)}, u32[]{:S(2)}) async-start(bf16[16,112,128]{2,1,0:T(8,128)(2,1)} %get-tuple-element.15), calls=%async_computation | async-start | bytes 917504 | tf_op jit(solution)/shard_map/all_to_all | solution.py:506
  27.1 11.8 %all-to-all-start.1 = ((bf16[16,96,128]{2,1,0:T(8,128)(2,1)}), bf16[16,96,128]{2,1,0:T(8,128)(2,1)S(1)}, u32[]{:S(2)}, u32[]{:S(2)}) async-start(bf16[16,96,128]{2,1,0:T(8,128)(2,1)} %get-tuple-element.16), calls=%async_computation.1 | async-start | bytes 786432 | tf_op jit(solution)/shard_map/all_to_all | solution.py:515
  45.2 4.0 %collective-permute-start = (f32[80,384]{1,0:T(8,128)S(1)}, f32[80,384]{1,0:T(8,128)S(1)}, u32[]{:S(2)}, u32[]{:S(2)}) collective-permute-start(f32[80,384]{1,0:T(8,128)S(1)} %get-tuple-element.18), channel_id=1, source_target_pairs={{0,1},{1,0},{2,3},{3,2},{4,5},{5,4},{6,7},{7,6},{8,9},{9,8},{10,11... | collective-permute-start | bytes 368648 | tf_op jit(solution)/shard_map/ppermute | solution.py:491
  73.3 2.8 %collective-permute-start.1 = (f32[80,384]{1,0:T(8,128)S(1)}, f32[80,384]{1,0:T(8,128)S(1)}, u32[]{:S(2)}, u32[]{:S(2)}) collective-permute-start(f32[80,384]{1,0:T(8,128)S(1)} %gather.1.mine), channel_id=1, source_target_pairs={{0,1},{1,0},{2,3},{3,2},{4,5},{5,4},{6,7},{7,6},{8,9},{9,8},{10,11... | collective-permute-start | bytes 368648 | tf_op jit(solution)/shard_map/ppermute | solution.py:491
  76.1 26.2 %copy-start.2 = (bf16[2,4,64,384]{3,2,1,0:T(8,128)(2,1)S(1)}, bf16[2,4,64,384]{3,2,1,0:T(8,128)(2,1)}, u32[]{:S(2)}) copy-start(bf16[2,4,64,384]{3,2,1,0:T(8,128)(2,1)} %tiles.3) | copy-start | bytes 1179652
  83.9 13.8 %all-to-all-start.3 = ((bf16[16,112,128]{2,1,0:T(8,128)(2,1)}), bf16[16,112,128]{2,1,0:T(8,128)(2,1)S(1)}, u32[]{:S(2)}, u32[]{:S(2)}) async-start(bf16[16,112,128]{2,1,0:T(8,128)(2,1)} %get-tuple-element.22), calls=%async_computation.3 | async-start | bytes 917504 | tf_op jit(solution)/shard_map/all_to_all | solution.py:545
  98.7 12.2 %all-to-all-start.4 = ((bf16[16,96,128]{2,1,0:T(8,128)(2,1)}), bf16[16,96,128]{2,1,0:T(8,128)(2,1)S(1)}, u32[]{:S(2)}, u32[]{:S(2)}) async-start(bf16[16,96,128]{2,1,0:T(8,128)(2,1)} %get-tuple-element.24), calls=%async_computation.4 | async-start | bytes 786432 | tf_op jit(solution)/shard_map/all_to_all | solution.py:554
  111.9 3.3 %collective-permute-start.2 = (f32[32,384]{1,0:T(8,128)S(1)}, f32[32,384]{1,0:T(8,128)S(1)}, u32[]{:S(2)}, u32[]{:S(2)}) collective-permute-start(f32[32,384]{1,0:T(8,128)S(1)} %pad_maximum_fusion.mine), channel_id=1, source_target_pairs={{0,1},{1,0},{2,3},{3,2},{4,5},{5,4},{6,7},{7,6},{8,9},{9,8},{10,11... | collective-permute-start | bytes 147464 | tf_op jit(solution)/shard_map/ppermute | solution.py:491

commit v3 on v2

--- a/solution.py
+++ b/solution.py
@@ -80,14 +80,17 @@
     return jnp.sum(total, axis=1, keepdims=True)
 
 
-def bands_of(source, target, done, first=0):
-    def copy(band):
-        at = pl.ds(pl.multiple_of(band * 16, 16), 16)
+def pieces_of(source, target, done, first=0):
+    groups = source.shape[1] // 8
+
+    def copy(band, group):
+        at = (slice(None), pl.ds(group * 8, 8), pl.ds(pl.multiple_of(band * BAND, BAND), BAND))
         return pltpu.make_async_copy(
-            source.at[:, :, at, :], target.at[:, :, at, :], done.at[first + band]
+            source.at[at], target.at[at], done.at[first + band * groups + group]
         )
 
-    return copy
+    copies = [copy(b, g) for b in range(source.shape[2] // BAND) for g in range(groups)]
+    return copy, copies
 
 
 def groups_of(source, target, done):
@@ -98,62 +101,70 @@
     return copy
 
 
-def send_points(series, tiles, copy, high, low, spec, out):
+def send_points(series, tiles, copy, high, low, spec, stage, out, gone):
     sens, points, freqs = tiles.shape[1:]
-    pair = product(series[...], high[...], low[...]) * frequency_weights(freqs)
-    spec[:, : 2 * freqs] = pair
-    spec[:, 2 * freqs :] = pair[:, :freqs] + pair[:, freqs:]
+    spec[...] = product(series[...], high[...], low[...]) * frequency_weights(freqs)
     blocks = freqs // LANES
-    step = 16
 
     def part(index, _):
         band = index // blocks
         block = index % blocks
-        lanes = [
-            pl.ds(pl.multiple_of(c * freqs + block * LANES, LANES), LANES) for c in range(3)
-        ]
-        range_ = pl.ds(pl.multiple_of(band * step, step), step)
-
-        @pl.when(block == 0)
-        def _():
-            copy(band).wait()
+        lanes = pl.ds(pl.multiple_of(block * LANES, LANES), LANES)
+        sines = pl.ds(pl.multiple_of(freqs + block * LANES, LANES), LANES)
+        range_ = pl.ds(pl.multiple_of(band * BAND, BAND), BAND)
 
         def group(g, acc):
+            @pl.when(block == 0)
+            def _():
+                copy(band, g).wait()
+
             acc = list(acc)
             rows = [pl.ds(pl.multiple_of(b * sens + g * 8, 8), 8) for b in range(REALS)]
-            values = [[spec[r, c] for c in lanes] for r in rows]
+            real = [spec[r, lanes] for r in rows]
+            imag = [spec[r, sines] for r in rows]
             for j in range(8):
-                tr = tiles[0, g * 8 + j, range_, lanes[0]].astype(F32)
-                ti = tiles[1, g * 8 + j, range_, lanes[0]].astype(F32)
-                terms = (tr, ti, tr - ti)
+                tr = tiles[0, g * 8 + j, range_, lanes].astype(F32)
+                ti = tiles[1, g * 8 + j, range_, lanes].astype(F32)
                 for b in range(REALS):
-                    acc[b] = tuple(
-                        acc[b][c] + values[b][c][j : j + 1] * terms[c] for c in range(3)
-                    )
+                    sr = real[b][j : j + 1]
+                    si = imag[b][j : j + 1]
+                    re, im = acc[b]
+                    acc[b] = (re + (sr * tr + si * ti), im + (si * tr - sr * ti))
             return tuple(acc)
 
-        zero = jnp.zeros((step, LANES), F32)
-        acc = lax.fori_loop(0, sens // 8, group, ((zero, zero, zero),) * REALS)
-        per = BAND // step
-        parts = points // BAND
-        at = pl.ds(pl.multiple_of(block * BAND + (band % per) * step, step), step)
+        zero = jnp.zeros((BAND, LANES), F32)
+        acc = lax.fori_loop(0, sens // 8, group, ((zero, zero),) * REALS)
+        rows = pl.ds(pl.multiple_of(block * BAND, BAND), BAND)
         for b in range(REALS):
-            first, second, third = acc[b]
-            out[b * parts + band // per, at, :] = (first + second).astype(BF16)
-            out[(REALS + b) * parts + band // per, at, :] = (third - first + second).astype(BF16)
+            for c in range(2):
+                stage[band * 2 * REALS + c * REALS + b, rows, :] = acc[b][c].astype(BF16)
+        send(index).start()
         return 0
 
-    lax.fori_loop(0, (points // step) * blocks, part, 0)
+    def send(index):
+        band = index // blocks
+        rows = pl.ds(pl.multiple_of((index % blocks) * BAND, BAND), BAND)
+        at = (pl.ds(band * 2 * REALS, 2 * REALS), rows)
+        return pltpu.make_async_copy(stage.at[at], out.at[at], gone.at[index])
+
+    number = (points // BAND) * blocks
+    at = (slice(None), pl.ds(blocks * BAND, EXTRA))
+    scalars = pltpu.make_async_copy(stage.at[at], out.at[at], gone.at[number])
+    scalars.start()
+    lax.fori_loop(0, number, part, 0)
+    for index in range(number):
+        send(index).wait()
+    scalars.wait()
 
 
 def first_kernel(
-    records, noise, tiles_in, high_in, low_in, out, series, column, raw, raw_noise, tiles, high, low, spec, done
+    records, noise, tiles_in, high_in, low_in, out, series, column, high, low, raw, raw_noise, tiles, spec, stage, done, gone
 ):
     reals, sens, steps = records.shape
     moves = ((records, raw), (noise, raw_noise), (high_in, high), (low_in, low))
     copies = [pltpu.make_async_copy(*move, done.at[k]) for k, move in enumerate(moves)]
-    fetch = bands_of(tiles_in, tiles, done, len(copies))
-    for copy in copies + [fetch(k) for k in range(tiles.shape[2] // 16)]:
+    fetch, pieces = pieces_of(tiles_in, tiles, done, len(copies))
+    for copy in copies + pieces:
         copy.start()
     copies[0].wait()
     copies[1].wait()
@@ -169,18 +180,18 @@
         values = series[b * sens : (b + 1) * sens, :]
         columns[0].append(band_sum(values, values, 0, sens))
         columns[1].append(band_sum(values, values * noises, 0, sens))
-    write_scalars(out, columns[0] + columns[1])
+    write_scalars(stage, columns[0] + columns[1])
     copies[2].wait()
     copies[3].wait()
-    send_points(series, tiles, fetch, high, low, spec, out)
+    send_points(series, tiles, fetch, high, low, spec, stage, out, gone)
 
 
 def second_kernel(
-    core, mine, theirs, series, noise, begin, tiles_in, high, low, out, residual, alpha, image, tiles, spec, done
+    core, mine, theirs, series, noise, begin, tiles_in, high, low, out, residual, alpha, image, tiles, spec, stage, done, gone
 ):
-    fetch = bands_of(tiles_in, tiles, done)
-    for k in range(tiles.shape[2] // 16):
-        fetch(k).start()
+    fetch, pieces = pieces_of(tiles_in, tiles, done)
+    for copy in pieces:
+        copy.start()
     half, freqs = mine.shape
     sens = 2 * half // REALS
     image[pl.ds(pl.multiple_of(core[0] * half, 8), half), :] = mine[...]
@@ -203,8 +214,8 @@
         columns[1].append(band_sum(left, left * noisy, 0, sens))
         columns[2].append(band_sum(left, values * noisy, 0, sens))
     alpha[...] = tile
-    write_scalars(out, columns[0] + columns[1] + columns[2])
-    send_points(residual, tiles, fetch, high, low, spec, out)
+    write_scalars(stage, columns[0] + columns[1] + columns[2])
+    send_points(residual, tiles, fetch, high, low, spec, stage, out, gone)
 
 
 def sum_message(got):
@@ -254,8 +265,8 @@
                 inverse = 1.0 / prior[h * BAND + row : h * BAND + row + 16, lanes]
                 for b in range(REALS):
                     at = slice(block * BAND + row, block * BAND + row + 16)
-                    re = weighted[b * parts + h, at, :].astype(F32)
-                    im = weighted[(REALS + b) * parts + h, at, :].astype(F32)
+                    re = weighted[h * 2 * REALS + b, at, :].astype(F32)
+                    im = weighted[h * 2 * REALS + REALS + b, at, :].astype(F32)
                     wide[b * parts + h, at, :] = re
                     wide[(REALS + b) * parts + h, at, :] = im
                     wide[(2 * REALS + b) * parts + h, at, :] = re + im
@@ -448,15 +459,14 @@
     return pltpu.with_memory_space_constraint(array, pltpu.HBM)
 
 
-def call(kernel, name, outs, scratch, specs, *args, semaphores=0, limit=24 * 2**20):
+def call(kernel, name, outs, scratch, specs, *args, send=False, semaphores=(), limit=24 * 2**20):
     scratch = [pltpu.VMEM(*one) for one in scratch]
     args = [in_hbm(arg) if spec is HBM else arg for arg, spec in zip(args, specs)]
-    if semaphores:
-        scratch.append(pltpu.SemaphoreType.DMA((semaphores,)))
+    scratch += [pltpu.SemaphoreType.DMA((number,)) for number in semaphores]
     return pl.pallas_call(
         kernel,
         in_specs=specs,
-        out_specs=[VMEM] * len(outs),
+        out_specs=[HBM if send and k == 0 else VMEM for k in range(len(outs))],
         out_shape=[jax.ShapeDtypeStruct(*out) for out in outs],
         scratch_shapes=scratch,
         compiler_params=pltpu.CompilerParams(vmem_limit_bytes=limit),
@@ -473,9 +483,9 @@
     heights = lax.axis_size("z")
     place = lax.axis_index("y") * lax.axis_size("x") + lax.axis_index("x")
     core = lax.axis_index("core").astype(jnp.int32).reshape(1)
-    start = lax.rem(place * BAND, points)
+    start = place // (2 * reals) * BAND
     prior_chunk = lax.dynamic_slice(prior, (start, 0), (BAND, freqs))
-    pick = lax.rem(place * BAND // points, reals).astype(jnp.int32).reshape(1)
+    pick = lax.rem(place, reals).astype(jnp.int32).reshape(1)
     count = reals * sensors
     half = count // 2
     block_rows = BAND * freqs // LANES
@@ -483,25 +493,24 @@
     weighted_shape = (senders, block_rows, LANES)
     wide_shape = (3 * senders // 2, block_rows, LANES)
     spectra = ((count, 2 * freqs), F32)
-    sums = ((count, 3 * freqs), F32)
     rows = ((count, freqs), F32)
     tile = ((8, LANES), F32)
 
     def swap(block):
         return lax.ppermute(block, "core", [(0, 1), (1, 0)])
 
-    bands = points // 16
+    bands = points // BAND
+    pieces = bands * (sensors // 8)
     local = (tiles.shape, BF16)
-    sent, series, noisy = call(
+    sent, series, noisy, *tables = call(
         first_kernel,
         "first",
-        [message, rows, ((sensors, 1), F32)],
-        [(records.shape, F32), ((1, sensors), F32), local]
-        + [(table.shape, BF16) for table in tables]
-        + [sums],
+        [message, rows, ((sensors, 1), F32)] + [(table.shape, BF16) for table in tables],
+        [(records.shape, F32), ((1, sensors), F32), local, spectra, message],
         [HBM] * 5,
         *(records, noise.reshape(1, sensors), tiles, *tables),
-        semaphores=4 + bands,
+        send=True,
+        semaphores=[4 + pieces, 7],
     )
     got = lax.all_to_all(sent, SENS, 0, 0)
     sent, points_0, begin = call(
@@ -520,7 +529,7 @@
         [(wide_shape, F32), spectra, rows, local],
         [SMEM, VMEM, VMEM, HBM, VMEM, VMEM],
         *(core, weighted_0, prior, tiles, *tables),
-        semaphores=sensors // 8,
+        semaphores=[sensors // 8],
     )
     (sent,) = call(
         functools.partial(spread_kernel, stride=8, begin=0),
@@ -537,10 +546,11 @@
         second_kernel,
         "second",
         [message, rows, tile],
-        [rows, local, sums],
+        [rows, local, spectra, message],
         [SMEM] + [VMEM] * 5 + [HBM, VMEM, VMEM],
         *(core, mine, theirs, series, noisy, begin, tiles, *tables),
-        semaphores=bands,
+        send=True,
+        semaphores=[pieces, 7],
     )
     got = lax.all_to_all(sent, SENS, 0, 0)
     sent, later = call(

time: 129 us -> 128 us (level)
  no operation moved by 1% of the time
where the time goes in v3:
time: 128 us
  waiting for transfers between devices  38.8 us (30%)
  blocking collectives  36.5 us (29%)
  Pallas kernels  26.1 us (20%)
  starting transfers between devices  25.6 us (20%)
    all_to_all x2, blocking collectives, on_device(): got = lax.all_to_all(sent, 'z', 0, 0)  36.5 us
    pallas_call x11, Pallas kernels, call(): pl.pallas_call(kernel, in_specs=specs, out_specs=[HBM if send and k == 0...  26.1 us
    all_to_all x2, waiting for transfers between devices, on_device(): got = lax.all_to_all(sent, SENS, 0, 0)  20.1 us
    all_to_all x2, starting transfers between devices, on_device(): got = lax.all_to_all(sent, SENS, 0, 0)  11.2 us
    all_to_all x1, waiting for transfers between devices, on_device(): weighted_0 = lax.all_to_all(sent, SENS, 0, 0)  8.23 us
    all_to_all x1, waiting for transfers between devices, on_device(): weighted_1 = lax.all_to_all(sent, SENS, 0, 0)  7.59 us
    ppermute x3, starting transfers between devices, swap(): return lax.ppermute(block, 'core', [(0, 1), (1, 0)])  7.32 us
    all_to_all x1, starting transfers between devices, on_device(): weighted_0 = lax.all_to_all(sent, SENS, 0, 0)  3.55 us
  transfers between devices with their start and end apart: 7, of which 7 were waited for; matrix products, arithmetic and copies ran while one was open for 0% of the time, Pallas kernels for 1%

profile of v3, /device:TPU:1, one launch (start us, length us, event | category | flops | bytes accessed | tf_op | source)
XLA Modules:
  0.0 127.7 jit_solution(10081905140630511251)
XLA Ops:
  0.6 0.0 copy-start.1
  0.6 7.9 %first.1 = (bf16[16,112,128]{2,1,0:T(8,128)(2,1)}, f32[160,384]{1,0:T(8,128)S(1)}, f32[40,1]{1,0:T(8,128)S(1)}, bf16[384,768]{1,0:T(8,128)(2,1)S(1)}, bf16[384,768]{1,0:T(8,128)(2,1)S(1)}) custom-call(f32[4,40,383]{2,1,0:T(8,128)} %records.1, f32[1,40]{1,0:T(1,128)} %bitcast.3, bf16[2,40,64,384]{3,2,1,0:T(8,128)(2,1)} %tiles_in.5, ...), custom_call_target="tpu_custom_call" | custom-call | tf_op jit(solution)/shard_map/first/pallas_call | solution.py:466
  8.5 7.6 %all-to-all-start = ((bf16[16,112,128]{2,1,0:T(8,128)(2,1)}), bf16[16,112,128]{2,1,0:T(8,128)(2,1)S(1)}, u32[]{:S(2)}, u32[]{:S(2)}) async-start(bf16[16,112,128]{2,1,0:T(8,128)(2,1)} %get-tuple-element.17), calls=%async_computation | async-start | bytes 917504 | tf_op jit(solution)/shard_map/all_to_all | solution.py:515
  16.2 0.0 copy-done.1
  16.2 9.9 %all-to-all-done.got = bf16[16,112,128]{2,1,0:T(8,128)(2,1)S(1)} async-done(((bf16[16,112,128]{2,1,0:T(8,128)(2,1)}), bf16[16,112,128]{2,1,0:T(8,128)(2,1)S(1)}, u32[]{:S(2)}, u32[]{:S(2)}) %all-to-all-start) | async-done | bytes 458784 | tf_op jit(solution)/shard_map/all_to_all | solution.py:515
  26.1 0.8 weigh.1
  26.9 3.6 %all-to-all-start.1 = ((bf16[16,96,128]{2,1,0:T(8,128)(2,1)}), bf16[16,96,128]{2,1,0:T(8,128)(2,1)S(1)}, u32[]{:S(2)}, u32[]{:S(2)}) async-start(bf16[16,96,128]{2,1,0:T(8,128)(2,1)} %get-tuple-element.18), calls=%async_computation.1 | async-start | bytes 786432 | tf_op jit(solution)/shard_map/all_to_all | solution.py:524
  30.5 8.2 %all-to-all-done.1.weighted = bf16[16,96,128]{2,1,0:T(8,128)(2,1)S(1)} async-done(((bf16[16,96,128]{2,1,0:T(8,128)(2,1)}), bf16[16,96,128]{2,1,0:T(8,128)(2,1)S(1)}, u32[]{:S(2)}, u32[]{:S(2)}) %all-to-all-start.1) | async-done | bytes 393248 | tf_op jit(solution)/shard_map/all_to_all | solution.py:524
  38.7 6.3 %forward.1 = (f32[80,384]{1,0:T(8,128)S(1)}, f32[80,384]{1,0:T(8,128)S(1)}) custom-call(s32[1]{0:T(128)} %bitcast.1.core, bf16[16,96,128]{2,1,0:T(8,128)(2,1)S(1)} %all-to-all-done.1.weighted, f32[64,384]{1,0:T(8,128)S(1)} %copy-done.1, bf16[2,40,64,384]{3,2,1,0:T(8,128)(2,1)} %tiles_in.5, bf16[384,768]{1,0:T(8,128)(2,1)S(1)} %get-tuple-element.19.high, ...), custom_call_target="tpu_custom_call" | custom-call | tf_op jit(solution)/shard_map/forward/pallas_call | solution.py:466
  45.0 3.0 %collective-permute-start = (f32[80,384]{1,0:T(8,128)S(1)}, f32[80,384]{1,0:T(8,128)S(1)}, u32[]{:S(2)}, u32[]{:S(2)}) collective-permute-start(f32[80,384]{1,0:T(8,128)S(1)} %get-tuple-element.22), channel_id=1, source_target_pairs={{0,1},{1,0},{2,3},{3,2},{4,5},{5,4},{6,7},{7,6},{8,9},{9,8},{10,11... | collective-permute-start | bytes 368648 | tf_op jit(solution)/shard_map/ppermute | solution.py:500
  48.0 1.0 collective-permute-done.got
  49.0 24.0 %all_to_all.30.got = bf16[8,80,384]{2,1,0:T(8,128)(2,1)S(1)} all-to-all(bf16[8,80,384]{2,1,0:T(8,128)(2,1)S(1)} %spread.1), channel_id=1, replica_groups=mesh['y'=4,'x'=4,'z'=8,'core'=2] {'z'}, dimensions={0} | all-to-all | bytes 983040 | tf_op jit(solution)/shard_map/all_to_all | solution.py:542
  73.0 0.1 gather.1.mine
  73.1 1.8 %collective-permute-start.1 = (f32[80,384]{1,0:T(8,128)S(1)}, f32[80,384]{1,0:T(8,128)S(1)}, u32[]{:S(2)}, u32[]{:S(2)}) collective-permute-start(f32[80,384]{1,0:T(8,128)S(1)} %gather.1.mine), channel_id=1, source_target_pairs={{0,1},{1,0},{2,3},{3,2},{4,5},{5,4},{6,7},{7,6},{8,9},{9,8},{10,11... | collective-permute-start | bytes 368648 | tf_op jit(solution)/shard_map/ppermute | solution.py:500
  74.9 1.0 collective-permute-done.1.theirs
  75.9 0.0 copy-start
  75.9 6.9 %second.1 = (bf16[16,112,128]{2,1,0:T(8,128)(2,1)}, f32[160,384]{1,0:T(8,128)S(1)}, f32[8,128]{1,0:T(8,128)S(1)}) custom-call(s32[1]{0:T(128)} %bitcast.1.core, f32[80,384]{1,0:T(8,128)S(1)} %gather.1.mine, f32[80,384]{1,0:T(8,128)S(1)} %collective-permute-done.1.theirs, f32[160,384]{1,0:T(8,128)S(1)} %get-tuple-element.23.series, ...), custom_call_target="tpu_custom_call" | custom-call | tf_op jit(solution)/shard_map/second/pallas_call | solution.py:466
  82.8 3.6 %all-to-all-start.3 = ((bf16[16,112,128]{2,1,0:T(8,128)(2,1)}), bf16[16,112,128]{2,1,0:T(8,128)(2,1)S(1)}, u32[]{:S(2)}, u32[]{:S(2)}) async-start(bf16[16,112,128]{2,1,0:T(8,128)(2,1)} %get-tuple-element.26), calls=%async_computation.3 | async-start | bytes 917504 | tf_op jit(solution)/shard_map/all_to_all | solution.py:555
  86.4 10.2 %all-to-all-done.3.got = bf16[16,112,128]{2,1,0:T(8,128)(2,1)S(1)} async-done(((bf16[16,112,128]{2,1,0:T(8,128)(2,1)}), bf16[16,112,128]{2,1,0:T(8,128)(2,1)S(1)}, u32[]{:S(2)}, u32[]{:S(2)}) %all-to-all-start.3) | async-done | bytes 458784 | tf_op jit(solution)/shard_map/all_to_all | solution.py:555
  96.6 1.0 weigh_next.1
  97.6 3.6 %all-to-all-start.4 = ((bf16[16,96,128]{2,1,0:T(8,128)(2,1)}), bf16[16,96,128]{2,1,0:T(8,128)(2,1)S(1)}, u32[]{:S(2)}, u32[]{:S(2)}) async-start(bf16[16,96,128]{2,1,0:T(8,128)(2,1)} %get-tuple-element.28), calls=%async_computation.4 | async-start | bytes 786432 | tf_op jit(solution)/shard_map/all_to_all | solution.py:564
  101.1 0.0 copy-done
  101.1 1.0 site_0.1
  102.2 7.6 %all-to-all-done.4.weighted = bf16[16,96,128]{2,1,0:T(8,128)(2,1)S(1)} async-done(((bf16[16,96,128]{2,1,0:T(8,128)(2,1)}), bf16[16,96,128]{2,1,0:T(8,128)(2,1)S(1)}, u32[]{:S(2)}, u32[]{:S(2)}) %all-to-all-start.4) | async-done | bytes 393248 | tf_op jit(solution)/shard_map/all_to_all | solution.py:564
  109.8 1.0 site_1.1
  110.8 2.5 %collective-permute-start.2 = (f32[32,384]{1,0:T(8,128)S(1)}, f32[32,384]{1,0:T(8,128)S(1)}, u32[]{:S(2)}, u32[]{:S(2)}) collective-permute-start(f32[32,384]{1,0:T(8,128)S(1)} %pad_maximum_fusion.mine), channel_id=1, source_target_pairs={{0,1},{1,0},{2,3},{3,2},{4,5},{5,4},{6,7},{7,6},{8,9},{9,8},{10,11... | collective-permute-start | bytes 147464 | tf_op jit(solution)/shard_map/ppermute | solution.py:500
  113.3 0.9 collective-permute-done.2.got
  114.2 12.5 %all_to_all.31.got = bf16[8,32,384]{2,1,0:T(8,128)(2,1)S(1)} all-to-all(bf16[8,32,384]{2,1,0:T(8,128)(2,1)S(1)} %spread_sites.1), channel_id=1, replica_groups=mesh['y'=4,'x'=4,'z'=8,'core'=2] {'z'}, dimensions={0} | all-to-all | bytes 393216 | tf_op jit(solution)/shard_map/all_to_all | solution.py:585
  126.7 1.0 last.1
  (4 shorter events, 0.1 us)
Async XLA Ops:
  0.6 15.5 %copy-start.1 = (f32[64,384]{1,0:T(8,128)S(1)}, f32[64,384]{1,0:T(8,128)}, u32[]{:S(2)}) copy-start(f32[64,384]{1,0:T(8,128)} %prior.5) | copy-start | bytes 294916
  8.5 17.5 %all-to-all-start = ((bf16[16,112,128]{2,1,0:T(8,128)(2,1)}), bf16[16,112,128]{2,1,0:T(8,128)(2,1)S(1)}, u32[]{:S(2)}, u32[]{:S(2)}) async-start(bf16[16,112,128]{2,1,0:T(8,128)(2,1)} %get-tuple-element.17), calls=%async_computation | async-start | bytes 917504 | tf_op jit(solution)/shard_map/all_to_all | solution.py:515
  26.9 11.8 %all-to-all-start.1 = ((bf16[16,96,128]{2,1,0:T(8,128)(2,1)}), bf16[16,96,128]{2,1,0:T(8,128)(2,1)S(1)}, u32[]{:S(2)}, u32[]{:S(2)}) async-start(bf16[16,96,128]{2,1,0:T(8,128)(2,1)} %get-tuple-element.18), calls=%async_computation.1 | async-start | bytes 786432 | tf_op jit(solution)/shard_map/all_to_all | solution.py:524
  45.0 4.0 %collective-permute-start = (f32[80,384]{1,0:T(8,128)S(1)}, f32[80,384]{1,0:T(8,128)S(1)}, u32[]{:S(2)}, u32[]{:S(2)}) collective-permute-start(f32[80,384]{1,0:T(8,128)S(1)} %get-tuple-element.22), channel_id=1, source_target_pairs={{0,1},{1,0},{2,3},{3,2},{4,5},{5,4},{6,7},{7,6},{8,9},{9,8},{10,11... | collective-permute-start | bytes 368648 | tf_op jit(solution)/shard_map/ppermute | solution.py:500
  73.1 2.8 %collective-permute-start.1 = (f32[80,384]{1,0:T(8,128)S(1)}, f32[80,384]{1,0:T(8,128)S(1)}, u32[]{:S(2)}, u32[]{:S(2)}) collective-permute-start(f32[80,384]{1,0:T(8,128)S(1)} %gather.1.mine), channel_id=1, source_target_pairs={{0,1},{1,0},{2,3},{3,2},{4,5},{5,4},{6,7},{7,6},{8,9},{9,8},{10,11... | collective-permute-start | bytes 368648 | tf_op jit(solution)/shard_map/ppermute | solution.py:500
  75.9 25.3 %copy-start = (bf16[2,4,64,384]{3,2,1,0:T(8,128)(2,1)S(1)}, bf16[2,4,64,384]{3,2,1,0:T(8,128)(2,1)}, u32[]{:S(2)}) copy-start(bf16[2,4,64,384]{3,2,1,0:T(8,128)(2,1)} %tiles.3) | copy-start | bytes 1179652
  82.8 13.8 %all-to-all-start.3 = ((bf16[16,112,128]{2,1,0:T(8,128)(2,1)}), bf16[16,112,128]{2,1,0:T(8,128)(2,1)S(1)}, u32[]{:S(2)}, u32[]{:S(2)}) async-start(bf16[16,112,128]{2,1,0:T(8,128)(2,1)} %get-tuple-element.26), calls=%async_computation.3 | async-start | bytes 917504 | tf_op jit(solution)/shard_map/all_to_all | solution.py:555
  97.6 12.2 %all-to-all-start.4 = ((bf16[16,96,128]{2,1,0:T(8,128)(2,1)}), bf16[16,96,128]{2,1,0:T(8,128)(2,1)S(1)}, u32[]{:S(2)}, u32[]{:S(2)}) async-start(bf16[16,96,128]{2,1,0:T(8,128)(2,1)} %get-tuple-element.28), calls=%async_computation.4 | async-start | bytes 786432 | tf_op jit(solution)/shard_map/all_to_all | solution.py:564
  110.8 3.3 %collective-permute-start.2 = (f32[32,384]{1,0:T(8,128)S(1)}, f32[32,384]{1,0:T(8,128)S(1)}, u32[]{:S(2)}, u32[]{:S(2)}) collective-permute-start(f32[32,384]{1,0:T(8,128)S(1)} %pad_maximum_fusion.mine), channel_id=1, source_target_pairs={{0,1},{1,0},{2,3},{3,2},{4,5},{5,4},{6,7},{7,6},{8,9},{9,8},{10,11... | collective-permute-start | bytes 147464 | tf_op jit(solution)/shard_map/ppermute | solution.py:500

commit v4 on v3

--- a/solution.py
+++ b/solution.py
@@ -101,7 +101,7 @@
     return copy
 
 
-def send_points(series, tiles, copy, high, low, spec, stage, out, gone):
+def send_points(series, tiles, copy, high, low, spec, out):
     sens, points, freqs = tiles.shape[1:]
     spec[...] = product(series[...], high[...], low[...]) * frequency_weights(freqs)
     blocks = freqs // LANES
@@ -137,28 +137,14 @@
         rows = pl.ds(pl.multiple_of(block * BAND, BAND), BAND)
         for b in range(REALS):
             for c in range(2):
-                stage[band * 2 * REALS + c * REALS + b, rows, :] = acc[b][c].astype(BF16)
-        send(index).start()
+                out[band * 2 * REALS + c * REALS + b, rows, :] = acc[b][c].astype(BF16)
         return 0
 
-    def send(index):
-        band = index // blocks
-        rows = pl.ds(pl.multiple_of((index % blocks) * BAND, BAND), BAND)
-        at = (pl.ds(band * 2 * REALS, 2 * REALS), rows)
-        return pltpu.make_async_copy(stage.at[at], out.at[at], gone.at[index])
-
-    number = (points // BAND) * blocks
-    at = (slice(None), pl.ds(blocks * BAND, EXTRA))
-    scalars = pltpu.make_async_copy(stage.at[at], out.at[at], gone.at[number])
-    scalars.start()
-    lax.fori_loop(0, number, part, 0)
-    for index in range(number):
-        send(index).wait()
-    scalars.wait()
+    lax.fori_loop(0, (points // BAND) * blocks, part, 0)
 
 
 def first_kernel(
-    records, noise, tiles_in, high_in, low_in, out, series, column, high, low, raw, raw_noise, tiles, spec, stage, done, gone
+    records, noise, tiles_in, high_in, low_in, out, series, column, high, low, raw, raw_noise, tiles, spec, done
 ):
     reals, sens, steps = records.shape
     moves = ((records, raw), (noise, raw_noise), (high_in, high), (low_in, low))
@@ -180,14 +166,14 @@
         values = series[b * sens : (b + 1) * sens, :]
         columns[0].append(band_sum(values, values, 0, sens))
         columns[1].append(band_sum(values, values * noises, 0, sens))
-    write_scalars(stage, columns[0] + columns[1])
+    write_scalars(out, columns[0] + columns[1])
     copies[2].wait()
     copies[3].wait()
-    send_points(series, tiles, fetch, high, low, spec, stage, out, gone)
+    send_points(series, tiles, fetch, high, low, spec, out)
 
 
 def second_kernel(
-    core, mine, theirs, series, noise, begin, tiles_in, high, low, out, residual, alpha, image, tiles, spec, stage, done, gone
+    core, mine, theirs, series, noise, begin, tiles_in, high, low, out, residual, alpha, image, tiles, spec, done
 ):
     fetch, pieces = pieces_of(tiles_in, tiles, done)
     for copy in pieces:
@@ -214,8 +200,8 @@
         columns[1].append(band_sum(left, left * noisy, 0, sens))
         columns[2].append(band_sum(left, values * noisy, 0, sens))
     alpha[...] = tile
-    write_scalars(stage, columns[0] + columns[1] + columns[2])
-    send_points(residual, tiles, fetch, high, low, spec, stage, out, gone)
+    write_scalars(out, columns[0] + columns[1] + columns[2])
+    send_points(residual, tiles, fetch, high, low, spec, out)
 
 
 def sum_message(got):
@@ -230,29 +216,30 @@
     return total, sums
 
 
-def put_weighted(total, prior, out):
+def put_weighted(total, prior, start, out):
+    points = pl.ds(pl.multiple_of(start[0], BAND), BAND)
     for block in range(prior.shape[1] // LANES):
         rows = slice(block * BAND, (block + 1) * BAND)
         lanes = slice(block * LANES, (block + 1) * LANES)
-        part = (total[rows] * prior[:, lanes]).astype(BF16)
+        part = (total[rows] * prior[points, lanes]).astype(BF16)
         for k in range(out.shape[0]):
             out[k, rows, :] = part
 
 
-def weigh_kernel(got, prior, out, kept, sums_out):
+def weigh_kernel(got, prior, start, out, kept, sums_out):
     total, sums = sum_message(got)
     kept[...] = total
     sums_out[...] = sums
-    put_weighted(total, prior, out)
-
-
-def weigh_next_kernel(got, prior, before, begin, pick, out, sums_out):
+    put_weighted(total, prior, start, out)
+
+
+def weigh_next_kernel(got, prior, before, begin, pick, start, out, sums_out):
     total, sums = sum_message(got)
     sums_out[...] = sums
     lane = lane_of((8, LANES))
     ratio = sums / jnp.where(lane < REALS, begin[...], 1.0)
     beta = jnp.sum(jnp.where(lane == pick[0], ratio, 0.0), axis=1, keepdims=True)[0:1]
-    put_weighted(total + beta * before[...], prior, out)
+    put_weighted(total + beta * before[...], prior, start, out)
 
 
 def widen(weighted, prior, wide):
@@ -459,14 +446,14 @@
     return pltpu.with_memory_space_constraint(array, pltpu.HBM)
 
 
-def call(kernel, name, outs, scratch, specs, *args, send=False, semaphores=(), limit=24 * 2**20):
+def call(kernel, name, outs, scratch, specs, *args, semaphores=(), limit=24 * 2**20):
     scratch = [pltpu.VMEM(*one) for one in scratch]
     args = [in_hbm(arg) if spec is HBM else arg for arg, spec in zip(args, specs)]
     scratch += [pltpu.SemaphoreType.DMA((number,)) for number in semaphores]
     return pl.pallas_call(
         kernel,
         in_specs=specs,
-        out_specs=[HBM if send and k == 0 else VMEM for k in range(len(outs))],
+        out_specs=[VMEM] * len(outs),
         out_shape=[jax.ShapeDtypeStruct(*out) for out in outs],
         scratch_shapes=scratch,
         compiler_params=pltpu.CompilerParams(vmem_limit_bytes=limit),
@@ -483,9 +470,11 @@
     heights = lax.axis_size("z")
     place = lax.axis_index("y") * lax.axis_size("x") + lax.axis_index("x")
     core = lax.axis_index("core").astype(jnp.int32).reshape(1)
-    start = place // (2 * reals) * BAND
-    prior_chunk = lax.dynamic_slice(prior, (start, 0), (BAND, freqs))
+    start = (place // (2 * reals) * BAND).astype(jnp.int32).reshape(1)
     pick = lax.rem(place, reals).astype(jnp.int32).reshape(1)
+    core, pick, start, prior, gauges, records = lax.optimization_barrier(
+        (core, pick, start, prior, gauges, records)
+    )
     count = reals * sensors
     half = count // 2
     block_rows = BAND * freqs // LANES
@@ -499,6 +488,16 @@
     def swap(block):
         return lax.ppermute(block, "core", [(0, 1), (1, 0)])
 
+    def site(weighted, name, tables):
+        return call(
+            site_kernel,
+            name,
+            [((reals * sites, freqs), F32)],
+            [(wide_shape, F32), ((reals * sites, 2 * freqs), F32)],
+            [VMEM] * 5,
+            *(weighted, prior, gauges, *tables),
+        )[0]
+
     bands = points // BAND
     pieces = bands * (sensors // 8)
     local = (tiles.shape, BF16)
@@ -506,11 +505,10 @@
         first_kernel,
         "first",
         [message, rows, ((sensors, 1), F32)] + [(table.shape, BF16) for table in tables],
-        [(records.shape, F32), ((1, sensors), F32), local, spectra, message],
+        [(records.shape, F32), ((1, sensors), F32), local, spectra],
         [HBM] * 5,
         *(records, noise.reshape(1, sensors), tiles, *tables),
-        send=True,
-        semaphores=[4 + pieces, 7],
+        semaphores=[4 + pieces],
     )
     got = lax.all_to_all(sent, SENS, 0, 0)
     sent, points_0, begin = call(
@@ -518,8 +516,8 @@
         "weigh",
         [(weighted_shape, BF16), ((block_rows, LANES), F32), tile],
         [],
-        [VMEM] * 2,
-        *(got, prior_chunk),
+        [VMEM, VMEM, SMEM],
+        *(got, prior, start),
     )
     weighted_0 = lax.all_to_all(sent, SENS, 0, 0)
     mine, other = call(
@@ -541,16 +539,17 @@
     )
     got = lax.all_to_all(sent, "z", 0, 0)
     (mine,) = call(sum_kernel, "gather", [((half, freqs), F32)], [], [VMEM], got)
-    theirs = swap(mine)
+    weighted_0, mine = lax.optimization_barrier((weighted_0, mine))
+    site_0 = site(weighted_0, "site_0", tables)
+    theirs, site_0 = lax.optimization_barrier((swap(mine), site_0))
     sent, residual, alpha = call(
         second_kernel,
         "second",
         [message, rows, tile],
-        [rows, local, spectra, message],
+        [rows, local, spectra],
         [SMEM] + [VMEM] * 5 + [HBM, VMEM, VMEM],
         *(core, mine, theirs, series, noisy, begin, tiles, *tables),
-        send=True,
-        semaphores=[pieces, 7],
+        semaphores=[pieces],
     )
     got = lax.all_to_all(sent, SENS, 0, 0)
     sent, later = call(
@@ -558,22 +557,12 @@
         "weigh_next",
         [(weighted_shape, BF16), tile],
         [],
-        [VMEM] * 4 + [SMEM],
-        *(got, prior_chunk, points_0, begin, pick),
+        [VMEM] * 4 + [SMEM] * 2,
+        *(got, prior, points_0, begin, pick, start),
     )
     weighted_1 = lax.all_to_all(sent, SENS, 0, 0)
 
-    def site(weighted, name):
-        return call(
-            site_kernel,
-            name,
-            [((reals * sites, freqs), F32)],
-            [(wide_shape, F32), ((reals * sites, 2 * freqs), F32)],
-            [VMEM] * 5,
-            *(weighted, prior, gauges, *tables),
-        )[0]
-
-    block = jnp.concatenate([site(weighted_0, "site_0"), site(weighted_1, "site_1")])
+    block = jnp.concatenate([site_0, site(weighted_1, "site_1", tables)])
     (sent,) = call(
         functools.partial(spread_kernel, stride=reals, begin=reals * sites),
         "spread_sites",

time: 128 us -> 123 us (0.961)
  blocking collectives: 36.5 us -> 89.7 us
  waiting for transfers between devices: 38.8 us -> 1.86 us
  starting transfers between devices: 25.6 us -> 7.18 us
  Pallas kernels: 26.1 us -> 23.2 us
    all_to_all x0 -> x4, blocking collectives: none -> 53.3 us  [the longest x2 30 us: on_device(): got = lax.all_to_all(sent, SENS, 0, 0)]
    all_to_all x4 -> x0, waiting for transfers between devices: 35.9 us -> none  [the longest x2 20.1 us: on_device(): got = lax.all_to_all(sent, SENS, 0, 0)]
    all_to_all x4 -> x0, starting transfers between devices: 18.3 us -> none  [the longest x2 11.2 us: on_device(): got = lax.all_to_all(sent, SENS, 0, 0)]
    pallas_call x11, Pallas kernels: 26.1 us -> 23.2 us  [call(): pl.pallas_call(kernel, in_specs=specs, out_specs=[VMEM] * len(outs), out_...]
  transfers between devices with their start and end apart: 7 -> 3, of which waited for: 7 -> 2; matrix products, arithmetic and copies ran while one was open for 0% -> 0% of each run, Pallas kernels for 1% -> 1%
where the time goes in v4:
time: 123 us
  blocking collectives  89.7 us (73%)
  Pallas kernels  23.2 us (19%)
  starting transfers between devices  7.18 us (6%)
  waiting for transfers between devices  1.86 us (2%)
    all_to_all x2, blocking collectives, on_device(): got = lax.all_to_all(sent, 'z', 0, 0)  36.5 us
    all_to_all x2, blocking collectives, on_device(): got = lax.all_to_all(sent, SENS, 0, 0)  30 us
    pallas_call x11, Pallas kernels, call(): pl.pallas_call(kernel, in_specs=specs, out_specs=[VMEM] * len(outs), out_...  23.2 us
    all_to_all x1, blocking collectives, on_device(): weighted_1 = lax.all_to_all(sent, SENS, 0, 0)  12.1 us
    all_to_all x1, blocking collectives, on_device(): weighted_0 = lax.all_to_all(sent, SENS, 0, 0)  11.2 us
    ppermute x3, starting transfers between devices, swap(): return lax.ppermute(block, 'core', [(0, 1), (1, 0)])  7.18 us
  transfers between devices with their start and end apart: 3, of which 2 were waited for; matrix products, arithmetic and copies ran while one was open for 0% of the time, Pallas kernels for 1%

profile of v4, /device:TPU:1, one launch (start us, length us, event | category | flops | bytes accessed | tf_op | source)
XLA Modules:
  0.0 122.7 jit_solution(11080020207380070270)
XLA Ops:
  0.6 0.0 copy-start
  0.7 7.2 %first.1 = (bf16[16,112,128]{2,1,0:T(8,128)(2,1)S(1)}, f32[160,384]{1,0:T(8,128)S(1)}, f32[40,1]{1,0:T(8,128)S(1)}, bf16[384,768]{1,0:T(8,128)(2,1)S(1)}, bf16[384,768]{1,0:T(8,128)(2,1)S(1)}) custom-call(f32[4,40,383]{2,1,0:T(8,128)} %records, f32[1,40]{1,0:T(1,128)} %bitcast.4, bf16[2,40,64,384]{3,2,1,0:T(8,128)(2,1)} %tiles_in.5, ...), custom_call_target="tpu_custom_call" | custom-call | tf_op jit(solution)/shard_map/first/pallas_call | solution.py:453
  7.9 17.3 %all_to_all.30.got = bf16[16,112,128]{2,1,0:T(8,128)(2,1)S(1)} all-to-all(bf16[16,112,128]{2,1,0:T(8,128)(2,1)S(1)} %get-tuple-element.28), channel_id=1, replica_groups=mesh['y'=4,'x'=4,'z'=8,'core'=2] {'y','x'}, dimensions={0} | all-to-all | bytes 917504 | tf_op jit(solution)/shard_map/all_to_all | solution.py:513
  25.2 0.0 copy-done
  25.2 0.1 weigh.1
  25.3 11.2 %all_to_all.31.weighted = bf16[16,96,128]{2,1,0:T(8,128)(2,1)S(1)} all-to-all(bf16[16,96,128]{2,1,0:T(8,128)(2,1)S(1)} %get-tuple-element.31), channel_id=1, replica_groups=mesh['y'=4,'x'=4,'z'=8,'core'=2] {'y','x'}, dimensions={0} | all-to-all | bytes 786432 | tf_op jit(solution)/shard_map/all_to_all | solution.py:522
  36.5 0.0 copy-start.1
  36.5 6.3 %forward.1 = (f32[80,384]{1,0:T(8,128)S(1)}, f32[80,384]{1,0:T(8,128)S(1)}) custom-call(s32[1]{0:T(128)} %bitcast.core, bf16[16,96,128]{2,1,0:T(8,128)(2,1)S(1)} %all_to_all.31.weighted, f32[64,384]{1,0:T(8,128)S(1)} %copy-done, bf16[2,40,64,384]{3,2,1,0:T(8,128)(2,1)} %tiles_in.5, bf16[384,768]{1,0:T(8,128)(2,1)S(1)} %get-tuple-element.33.high, ...), custom_call_target="tpu_custom_call" | custom-call | tf_op jit(solution)/shard_map/forward/pallas_call | solution.py:453
  42.8 3.0 %collective-permute-start = (f32[80,384]{1,0:T(8,128)S(1)}, f32[80,384]{1,0:T(8,128)S(1)}, u32[]{:S(2)}, u32[]{:S(2)}) collective-permute-start(f32[80,384]{1,0:T(8,128)S(1)} %get-tuple-element.36), channel_id=1, source_target_pairs={{0,1},{1,0},{2,3},{3,2},{4,5},{5,4},{6,7},{7,6},{8,9},{9,8},{10,11... | collective-permute-start | bytes 368648 | tf_op jit(solution)/shard_map/ppermute | solution.py:489
  45.8 1.0 collective-permute-done.got
  46.8 24.0 %all_to_all.32.got = bf16[8,80,384]{2,1,0:T(8,128)(2,1)S(1)} all-to-all(bf16[8,80,384]{2,1,0:T(8,128)(2,1)S(1)} %spread.1), channel_id=1, replica_groups=mesh['y'=4,'x'=4,'z'=8,'core'=2] {'z'}, dimensions={0} | all-to-all | bytes 983040 | tf_op jit(solution)/shard_map/all_to_all | solution.py:540
  70.8 0.1 gather.1.mine
  70.9 1.8 %collective-permute-start.1 = (f32[80,384]{1,0:T(8,128)S(1)}, f32[80,384]{1,0:T(8,128)S(1)}, u32[]{:S(2)}, u32[]{:S(2)}) collective-permute-start(f32[80,384]{1,0:T(8,128)S(1)} %gather.1.mine), channel_id=1, source_target_pairs={{0,1},{1,0},{2,3},{3,2},{4,5},{5,4},{6,7},{7,6},{8,9},{9,8},{10,11... | collective-permute-start | bytes 368648 | tf_op jit(solution)/shard_map/ppermute | solution.py:489
  72.7 0.0 copy-done.1
  72.7 1.0 site_0.1
  73.8 0.0 collective-permute-done.1.theirs
  73.8 6.2 %second.1 = (bf16[16,112,128]{2,1,0:T(8,128)(2,1)S(1)}, f32[160,384]{1,0:T(8,128)S(1)}, f32[8,128]{1,0:T(8,128)S(1)}) custom-call(s32[1]{0:T(128)} %bitcast.core, f32[80,384]{1,0:T(8,128)S(1)} %gather.1.mine, f32[80,384]{1,0:T(8,128)S(1)} %collective-permute-done.1.theirs, f32[160,384]{1,0:T(8,128)S(1)} %get-tuple-element.42.series, ...), custom_call_target="tpu_custom_call" | custom-call | tf_op jit(solution)/shard_map/second/pallas_call | solution.py:453
  80.0 12.7 %all_to_all.33.got = bf16[16,112,128]{2,1,0:T(8,128)(2,1)S(1)} all-to-all(bf16[16,112,128]{2,1,0:T(8,128)(2,1)S(1)} %get-tuple-element.45), channel_id=1, replica_groups=mesh['y'=4,'x'=4,'z'=8,'core'=2] {'y','x'}, dimensions={0} | all-to-all | bytes 917504 | tf_op jit(solution)/shard_map/all_to_all | solution.py:554
  92.6 0.2 weigh_next.1
  92.8 12.1 %all_to_all.34.weighted = bf16[16,96,128]{2,1,0:T(8,128)(2,1)S(1)} all-to-all(bf16[16,96,128]{2,1,0:T(8,128)(2,1)S(1)} %get-tuple-element.48), channel_id=1, replica_groups=mesh['y'=4,'x'=4,'z'=8,'core'=2] {'y','x'}, dimensions={0} | all-to-all | bytes 786432 | tf_op jit(solution)/shard_map/all_to_all | solution.py:563
  104.9 1.0 site_1.1
  105.9 2.3 %collective-permute-start.2 = (f32[32,384]{1,0:T(8,128)S(1)}, f32[32,384]{1,0:T(8,128)S(1)}, u32[]{:S(2)}, u32[]{:S(2)}) collective-permute-start(f32[32,384]{1,0:T(8,128)S(1)} %pad_maximum_fusion.mine), channel_id=1, source_target_pairs={{0,1},{1,0},{2,3},{3,2},{4,5},{5,4},{6,7},{7,6},{8,9},{9,8},{10,11... | collective-permute-start | bytes 147464 | tf_op jit(solution)/shard_map/ppermute | solution.py:489
  108.3 0.9 collective-permute-done.2.got
  109.2 12.5 %all_to_all.35.got = bf16[8,32,384]{2,1,0:T(8,128)(2,1)S(1)} all-to-all(bf16[8,32,384]{2,1,0:T(8,128)(2,1)S(1)} %spread_sites.1), channel_id=1, replica_groups=mesh['y'=4,'x'=4,'z'=8,'core'=2] {'z'}, dimensions={0} | all-to-all | bytes 393216 | tf_op jit(solution)/shard_map/all_to_all | solution.py:574
  121.7 1.0 last.1
  (3 shorter events, 0.1 us)
Async XLA Ops:
  0.6 24.5 %copy-start = (f32[64,384]{1,0:T(8,128)S(1)}, f32[64,384]{1,0:T(8,128)}, u32[]{:S(2)}) copy-start(f32[64,384]{1,0:T(8,128)} %prior.4) | copy-start | bytes 294916
  36.5 36.2 %copy-start.1 = (bf16[2,4,64,384]{3,2,1,0:T(8,128)(2,1)S(1)}, bf16[2,4,64,384]{3,2,1,0:T(8,128)(2,1)}, u32[]{:S(2)}) copy-start(bf16[2,4,64,384]{3,2,1,0:T(8,128)(2,1)} %tiles.1) | copy-start | bytes 1179652
  42.8 4.0 %collective-permute-start = (f32[80,384]{1,0:T(8,128)S(1)}, f32[80,384]{1,0:T(8,128)S(1)}, u32[]{:S(2)}, u32[]{:S(2)}) collective-permute-start(f32[80,384]{1,0:T(8,128)S(1)} %get-tuple-element.36), channel_id=1, source_target_pairs={{0,1},{1,0},{2,3},{3,2},{4,5},{5,4},{6,7},{7,6},{8,9},{9,8},{10,11... | collective-permute-start | bytes 368648 | tf_op jit(solution)/shard_map/ppermute | solution.py:489
  70.9 2.9 %collective-permute-start.1 = (f32[80,384]{1,0:T(8,128)S(1)}, f32[80,384]{1,0:T(8,128)S(1)}, u32[]{:S(2)}, u32[]{:S(2)}) collective-permute-start(f32[80,384]{1,0:T(8,128)S(1)} %gather.1.mine), channel_id=1, source_target_pairs={{0,1},{1,0},{2,3},{3,2},{4,5},{5,4},{6,7},{7,6},{8,9},{9,8},{10,11... | collective-permute-start | bytes 368648 | tf_op jit(solution)/shard_map/ppermute | solution.py:489
  105.9 3.2 %collective-permute-start.2 = (f32[32,384]{1,0:T(8,128)S(1)}, f32[32,384]{1,0:T(8,128)S(1)}, u32[]{:S(2)}, u32[]{:S(2)}) collective-permute-start(f32[32,384]{1,0:T(8,128)S(1)} %pad_maximum_fusion.mine), channel_id=1, source_target_pairs={{0,1},{1,0},{2,3},{3,2},{4,5},{5,4},{6,7},{7,6},{8,9},{9,8},{10,11... | collective-permute-start | bytes 147464 | tf_op jit(solution)/shard_map/ppermute | solution.py:489

commit v5 on v4

--- a/solution.py
+++ b/solution.py
@@ -14,7 +14,7 @@
 REALS = 4
 LANES = 128
 BAND = 32
-EXTRA = 16
+EXTRA = 8
 F32 = jnp.float32
 BF16 = jnp.bfloat16
 VMEM = pl.BlockSpec(memory_space=pltpu.VMEM)
@@ -67,7 +67,7 @@
         tile = jnp.where(lane == k, column, tile)
     first, second, third = three(tile)
     tile = first + pltpu.roll(second, 32, 1) + pltpu.roll(third, 64, 1)
-    block = jnp.concatenate([tile, jnp.zeros_like(tile)]).astype(BF16)
+    block = tile.astype(BF16)
     rows = out.shape[1] - EXTRA
     for k in range(out.shape[0]):
         out[k, rows:, :] = block
@@ -103,7 +103,8 @@
 
 def send_points(series, tiles, copy, high, low, spec, out):
     sens, points, freqs = tiles.shape[1:]
-    spec[...] = product(series[...], high[...], low[...]) * frequency_weights(freqs)
+    pair = product(series[...], high[...], low[...]) * frequency_weights(freqs)
+    spec[...] = pair.reshape(spec.shape)
     blocks = freqs // LANES
 
     def part(index, _):
@@ -119,15 +120,13 @@
                 copy(band, g).wait()
 
             acc = list(acc)
-            rows = [pl.ds(pl.multiple_of(b * sens + g * 8, 8), 8) for b in range(REALS)]
-            real = [spec[r, lanes] for r in rows]
-            imag = [spec[r, sines] for r in rows]
+            rows = [b * (sens // 8) + g for b in range(REALS)]
             for j in range(8):
                 tr = tiles[0, g * 8 + j, range_, lanes].astype(F32)
                 ti = tiles[1, g * 8 + j, range_, lanes].astype(F32)
                 for b in range(REALS):
-                    sr = real[b][j : j + 1]
-                    si = imag[b][j : j + 1]
+                    sr = spec[rows[b], j : j + 1, lanes]
+                    si = spec[rows[b], j : j + 1, sines]
                     re, im = acc[b]
                     acc[b] = (re + (sr * tr + si * ti), im + (si * tr - sr * ti))
             return tuple(acc)
@@ -481,7 +480,8 @@
     message = ((senders, block_rows + EXTRA, LANES), BF16)
     weighted_shape = (senders, block_rows, LANES)
     wide_shape = (3 * senders // 2, block_rows, LANES)
-    spectra = ((count, 2 * freqs), F32)
+    spectra = ((count // 8, 8, 2 * freqs), F32)
+    flat = ((count, 2 * freqs), F32)
     rows = ((count, freqs), F32)
     tile = ((8, LANES), F32)
 
@@ -524,7 +524,7 @@
         forward_kernel,
         "forward",
         [((half, freqs), F32)] * 2,
-        [(wide_shape, F32), spectra, rows, local],
+        [(wide_shape, F32), flat, rows, local],
         [SMEM, VMEM, VMEM, HBM, VMEM, VMEM],
         *(core, weighted_0, prior, tiles, *tables),
         semaphores=[sensors // 8],

time: 123 us -> 122 us (level)
  no operation moved by 1% of the time
where the time goes in v5:
time: 122 us; the launch traced here: 121 us
  blocking collectives  88.9 us (73%)
  Pallas kernels  22.6 us (19%)
  starting transfers between devices  7.24 us (6%)
  waiting for transfers between devices  1.86 us (2%)
    all_to_all x2, blocking collectives, on_device(): got = lax.all_to_all(sent, 'z', 0, 0)  36.5 us
    all_to_all x2, blocking collectives, on_device(): got = lax.all_to_all(sent, SENS, 0, 0)  29.3 us
    pallas_call x11, Pallas kernels, call(): pl.pallas_call(kernel, in_specs=specs, out_specs=[VMEM] * len(outs), out_...  22.6 us
    all_to_all x1, blocking collectives, on_device(): weighted_1 = lax.all_to_all(sent, SENS, 0, 0)  12 us
    all_to_all x1, blocking collectives, on_device(): weighted_0 = lax.all_to_all(sent, SENS, 0, 0)  11.2 us
    ppermute x3, starting transfers between devices, swap(): return lax.ppermute(block, 'core', [(0, 1), (1, 0)])  7.24 us
  transfers between devices with their start and end apart: 3, of which 2 were waited for; matrix products, arithmetic and copies ran while one was open for 0% of the time, Pallas kernels for 1%

profile of v5, /device:TPU:1, one launch (start us, length us, event | category | flops | bytes accessed | tf_op | source)
XLA Modules:
  0.0 121.4 jit_solution(10828636465732713349)
XLA Ops:
  0.6 0.0 copy-start
  0.7 6.9 %first.1 = (bf16[16,104,128]{2,1,0:T(8,128)(2,1)S(1)}, f32[160,384]{1,0:T(8,128)S(1)}, f32[40,1]{1,0:T(8,128)S(1)}, bf16[384,768]{1,0:T(8,128)(2,1)S(1)}, bf16[384,768]{1,0:T(8,128)(2,1)S(1)}) custom-call(f32[4,40,383]{2,1,0:T(8,128)} %records, f32[1,40]{1,0:T(1,128)} %bitcast.4, bf16[2,40,64,384]{3,2,1,0:T(8,128)(2,1)} %tiles_in.5, ...), custom_call_target="tpu_custom_call" | custom-call | tf_op jit(solution)/shard_map/first/pallas_call | solution.py:452
  7.6 16.9 %all_to_all.30.got = bf16[16,104,128]{2,1,0:T(8,128)(2,1)S(1)} all-to-all(bf16[16,104,128]{2,1,0:T(8,128)(2,1)S(1)} %get-tuple-element.28), channel_id=1, replica_groups=mesh['y'=4,'x'=4,'z'=8,'core'=2] {'y','x'}, dimensions={0} | all-to-all | bytes 851968 | tf_op jit(solution)/shard_map/all_to_all | solution.py:513
  24.5 0.0 copy-done
  24.5 0.1 weigh.1
  24.6 11.2 %all_to_all.31.weighted = bf16[16,96,128]{2,1,0:T(8,128)(2,1)S(1)} all-to-all(bf16[16,96,128]{2,1,0:T(8,128)(2,1)S(1)} %get-tuple-element.31), channel_id=1, replica_groups=mesh['y'=4,'x'=4,'z'=8,'core'=2] {'y','x'}, dimensions={0} | all-to-all | bytes 786432 | tf_op jit(solution)/shard_map/all_to_all | solution.py:522
  35.8 0.0 copy-start.1
  35.8 6.3 %forward.1 = (f32[80,384]{1,0:T(8,128)S(1)}, f32[80,384]{1,0:T(8,128)S(1)}) custom-call(s32[1]{0:T(128)} %bitcast.core, bf16[16,96,128]{2,1,0:T(8,128)(2,1)S(1)} %all_to_all.31.weighted, f32[64,384]{1,0:T(8,128)S(1)} %copy-done, bf16[2,40,64,384]{3,2,1,0:T(8,128)(2,1)} %tiles_in.5, bf16[384,768]{1,0:T(8,128)(2,1)S(1)} %get-tuple-element.33.high, ...), custom_call_target="tpu_custom_call" | custom-call | tf_op jit(solution)/shard_map/forward/pallas_call | solution.py:452
  42.1 3.0 %collective-permute-start = (f32[80,384]{1,0:T(8,128)S(1)}, f32[80,384]{1,0:T(8,128)S(1)}, u32[]{:S(2)}, u32[]{:S(2)}) collective-permute-start(f32[80,384]{1,0:T(8,128)S(1)} %get-tuple-element.36), channel_id=1, source_target_pairs={{0,1},{1,0},{2,3},{3,2},{4,5},{5,4},{6,7},{7,6},{8,9},{9,8},{10,11... | collective-permute-start | bytes 368648 | tf_op jit(solution)/shard_map/ppermute | solution.py:489
  45.2 1.0 collective-permute-done.got
  46.2 24.0 %all_to_all.32.got = bf16[8,80,384]{2,1,0:T(8,128)(2,1)S(1)} all-to-all(bf16[8,80,384]{2,1,0:T(8,128)(2,1)S(1)} %spread.1), channel_id=1, replica_groups=mesh['y'=4,'x'=4,'z'=8,'core'=2] {'z'}, dimensions={0} | all-to-all | bytes 983040 | tf_op jit(solution)/shard_map/all_to_all | solution.py:540
  70.2 0.1 gather.1.mine
  70.2 1.8 %collective-permute-start.1 = (f32[80,384]{1,0:T(8,128)S(1)}, f32[80,384]{1,0:T(8,128)S(1)}, u32[]{:S(2)}, u32[]{:S(2)}) collective-permute-start(f32[80,384]{1,0:T(8,128)S(1)} %gather.1.mine), channel_id=1, source_target_pairs={{0,1},{1,0},{2,3},{3,2},{4,5},{5,4},{6,7},{7,6},{8,9},{9,8},{10,11... | collective-permute-start | bytes 368648 | tf_op jit(solution)/shard_map/ppermute | solution.py:489
  72.1 0.0 copy-done.1
  72.1 1.0 site_0.1
  73.1 0.0 collective-permute-done.1.theirs
  73.1 5.9 %second.1 = (bf16[16,104,128]{2,1,0:T(8,128)(2,1)S(1)}, f32[160,384]{1,0:T(8,128)S(1)}, f32[8,128]{1,0:T(8,128)S(1)}) custom-call(s32[1]{0:T(128)} %bitcast.core, f32[80,384]{1,0:T(8,128)S(1)} %gather.1.mine, f32[80,384]{1,0:T(8,128)S(1)} %collective-permute-done.1.theirs, f32[160,384]{1,0:T(8,128)S(1)} %get-tuple-element.42.series, ...), custom_call_target="tpu_custom_call" | custom-call | tf_op jit(solution)/shard_map/second/pallas_call | solution.py:452
  79.0 12.3 %all_to_all.33.got = bf16[16,104,128]{2,1,0:T(8,128)(2,1)S(1)} all-to-all(bf16[16,104,128]{2,1,0:T(8,128)(2,1)S(1)} %get-tuple-element.45), channel_id=1, replica_groups=mesh['y'=4,'x'=4,'z'=8,'core'=2] {'y','x'}, dimensions={0} | all-to-all | bytes 851968 | tf_op jit(solution)/shard_map/all_to_all | solution.py:554
  91.3 0.2 weigh_next.1
  91.5 12.0 %all_to_all.34.weighted = bf16[16,96,128]{2,1,0:T(8,128)(2,1)S(1)} all-to-all(bf16[16,96,128]{2,1,0:T(8,128)(2,1)S(1)} %get-tuple-element.48), channel_id=1, replica_groups=mesh['y'=4,'x'=4,'z'=8,'core'=2] {'y','x'}, dimensions={0} | all-to-all | bytes 786432 | tf_op jit(solution)/shard_map/all_to_all | solution.py:563
  103.5 1.0 site_1.1
  104.6 2.4 %collective-permute-start.2 = (f32[32,384]{1,0:T(8,128)S(1)}, f32[32,384]{1,0:T(8,128)S(1)}, u32[]{:S(2)}, u32[]{:S(2)}) collective-permute-start(f32[32,384]{1,0:T(8,128)S(1)} %pad_maximum_fusion.mine), channel_id=1, source_target_pairs={{0,1},{1,0},{2,3},{3,2},{4,5},{5,4},{6,7},{7,6},{8,9},{9,8},{10,11... | collective-permute-start | bytes 147464 | tf_op jit(solution)/shard_map/ppermute | solution.py:489
  106.9 0.9 collective-permute-done.2.got
  107.8 12.5 %all_to_all.35.got = bf16[8,32,384]{2,1,0:T(8,128)(2,1)S(1)} all-to-all(bf16[8,32,384]{2,1,0:T(8,128)(2,1)S(1)} %spread_sites.1), channel_id=1, replica_groups=mesh['y'=4,'x'=4,'z'=8,'core'=2] {'z'}, dimensions={0} | all-to-all | bytes 393216 | tf_op jit(solution)/shard_map/all_to_all | solution.py:574
  120.3 1.0 last.1
  (3 shorter events, 0.1 us)
Async XLA Ops:
  0.6 23.9 %copy-start = (f32[64,384]{1,0:T(8,128)S(1)}, f32[64,384]{1,0:T(8,128)}, u32[]{:S(2)}) copy-start(f32[64,384]{1,0:T(8,128)} %prior.4) | copy-start | bytes 294916
  35.8 36.3 %copy-start.1 = (bf16[2,4,64,384]{3,2,1,0:T(8,128)(2,1)S(1)}, bf16[2,4,64,384]{3,2,1,0:T(8,128)(2,1)}, u32[]{:S(2)}) copy-start(bf16[2,4,64,384]{3,2,1,0:T(8,128)(2,1)} %tiles.1) | copy-start | bytes 1179652
  42.1 4.0 %collective-permute-start = (f32[80,384]{1,0:T(8,128)S(1)}, f32[80,384]{1,0:T(8,128)S(1)}, u32[]{:S(2)}, u32[]{:S(2)}) collective-permute-start(f32[80,384]{1,0:T(8,128)S(1)} %get-tuple-element.36), channel_id=1, source_target_pairs={{0,1},{1,0},{2,3},{3,2},{4,5},{5,4},{6,7},{7,6},{8,9},{9,8},{10,11... | collective-permute-start | bytes 368648 | tf_op jit(solution)/shard_map/ppermute | solution.py:489
  70.2 2.9 %collective-permute-start.1 = (f32[80,384]{1,0:T(8,128)S(1)}, f32[80,384]{1,0:T(8,128)S(1)}, u32[]{:S(2)}, u32[]{:S(2)}) collective-permute-start(f32[80,384]{1,0:T(8,128)S(1)} %gather.1.mine), channel_id=1, source_target_pairs={{0,1},{1,0},{2,3},{3,2},{4,5},{5,4},{6,7},{7,6},{8,9},{9,8},{10,11... | collective-permute-start | bytes 368648 | tf_op jit(solution)/shard_map/ppermute | solution.py:489
  104.6 3.2 %collective-permute-start.2 = (f32[32,384]{1,0:T(8,128)S(1)}, f32[32,384]{1,0:T(8,128)S(1)}, u32[]{:S(2)}, u32[]{:S(2)}) collective-permute-start(f32[32,384]{1,0:T(8,128)S(1)} %pad_maximum_fusion.mine), channel_id=1, source_target_pairs={{0,1},{1,0},{2,3},{3,2},{4,5},{5,4},{6,7},{7,6},{8,9},{9,8},{10,11... | collective-permute-start | bytes 147464 | tf_op jit(solution)/shard_map/ppermute | solution.py:489

commit v6 on v5

--- a/solution.py
+++ b/solution.py
@@ -39,14 +39,18 @@
     return jnp.where((at == 0) | (at == freqs - 1), 1.0 / padded, 2.0 / padded)
 
 
-def product(left, high, low):
+def product(left, high, low, ready=None):
+    rows = left.shape[0]
     first = left.astype(BF16)
     second = (left - first.astype(F32)).astype(BF16)
 
     def dot(a, b):
         return jnp.dot(a, b, preferred_element_type=F32)
 
-    return dot(first, high) + (dot(first, low) + dot(second, high))
+    both = dot(jnp.concatenate([first, second]), high[...])
+    if ready is not None:
+        ready()
+    return both[:rows] + (dot(first, low[...]) + both[rows:])
 
 
 def lane_of(shape):
@@ -101,9 +105,9 @@
     return copy
 
 
-def send_points(series, tiles, copy, high, low, spec, out):
+def send_points(series, tiles, copy, high, low, spec, out, ready=None):
     sens, points, freqs = tiles.shape[1:]
-    pair = product(series[...], high[...], low[...]) * frequency_weights(freqs)
+    pair = product(series[...], high, low, ready) * frequency_weights(freqs)
     spec[...] = pair.reshape(spec.shape)
     blocks = freqs // LANES
 
@@ -143,13 +147,19 @@
 
 
 def first_kernel(
-    records, noise, tiles_in, high_in, low_in, out, series, column, high, low, raw, raw_noise, tiles, spec, done
+    records, noise, tiles_in, high_in, low_in, out, series, column, high, low, head, raw, raw_noise, tiles, spec, done
 ):
     reals, sens, steps = records.shape
-    moves = ((records, raw), (noise, raw_noise), (high_in, high), (low_in, low))
+    moves = (
+        (records, raw),
+        (noise, raw_noise),
+        (high_in, high),
+        (low_in, low),
+        (tiles_in.at[:, :8], head),
+    )
     copies = [pltpu.make_async_copy(*move, done.at[k]) for k, move in enumerate(moves)]
     fetch, pieces = pieces_of(tiles_in, tiles, done, len(copies))
-    for copy in copies + pieces:
+    for copy in copies[:4] + pieces + copies[4:]:
         copy.start()
     copies[0].wait()
     copies[1].wait()
@@ -167,8 +177,8 @@
         columns[1].append(band_sum(values, values * noises, 0, sens))
     write_scalars(out, columns[0] + columns[1])
     copies[2].wait()
-    copies[3].wait()
-    send_points(series, tiles, fetch, high, low, spec, out)
+    send_points(series, tiles, fetch, high, low, spec, out, copies[3].wait)
+    copies[4].wait()
 
 
 def second_kernel(
@@ -297,8 +307,8 @@
 def synthesize(rows, high, low, energy, stride):
     count, freqs = rows.shape[0], rows.shape[1] // 2
     scaled = rows[...] * frequency_weights(freqs)
-    series = product(scaled[:, :freqs], high[:, :freqs], low[:, :freqs]) + product(
-        scaled[:, freqs:], high[:, freqs:], low[:, freqs:]
+    series = product(scaled[:, :freqs], high.at[:, :freqs], low.at[:, :freqs]) + product(
+        scaled[:, freqs:], high.at[:, freqs:], low.at[:, freqs:]
     )
     row = lax.broadcasted_iota(jnp.int32, (count, freqs), 0)
     lane = lane_of((count, freqs))
@@ -311,28 +321,26 @@
 
 
 def forward_kernel(
-    core, weighted, prior, tiles_in, high, low, mine, other, wide, rows, full, tiles, done
+    core, weighted, prior, head, tiles_in, high, low, mine, other, wide, rows, full, tiles, done
 ):
     sens, points, freqs = tiles.shape[1:]
     fetch = groups_of(tiles_in, tiles, done)
-    for k in range(sens // 8):
+    for k in range(1, sens // 8):
         fetch(k).start()
     energy = widen(weighted, prior, wide)
     place = lax.broadcasted_iota(jnp.int32, (8, LANES), 0)
     blocks = freqs // LANES
 
-    def part(index, _):
+    def part(index, source, begin):
         g = index // blocks
         block = index % blocks
         lanes = pl.ds(pl.multiple_of(block * LANES, LANES), LANES)
         sines = pl.ds(pl.multiple_of(freqs + block * LANES, LANES), LANES)
-
-        @pl.when(block == 0)
-        def _():
-            fetch(g).wait()
+        base = begin * 8
 
         def pair(k):
-            sums = site_sums(tiles, wide, [g * 8 + k, g * 8 + k + 4], range(REALS), block, lanes)
+            sensors = [base + k, base + k + 4]
+            sums = site_sums(source, wide, sensors, range(REALS), block, lanes)
             return [
                 [merge(sums[0, b][c], sums[1, b][c], 4, place) for c in range(2)]
                 for b in range(REALS)
@@ -354,7 +362,20 @@
             rows[at, sines] = merge(first[b][1], second[b][1], 1, place)
         return 0
 
-    lax.fori_loop(0, (sens // 8) * blocks, part, 0)
+    def head_part(index, _):
+        return part(index, head, 0)
+
+    def tile_part(index, _):
+        group = index // blocks
+
+        @pl.when(index % blocks == 0)
+        def _():
+            fetch(group).wait()
+
+        return part(index, tiles, group)
+
+    lax.fori_loop(0, blocks, head_part, 0)
+    lax.fori_loop(blocks, (sens // 8) * blocks, tile_part, 0)
     half = REALS * sens // 2
     series = synthesize(rows, high, low, energy + energy, 8)
     row = lax.broadcasted_iota(jnp.int32, (half, freqs), 0)
@@ -501,14 +522,16 @@
     bands = points // BAND
     pieces = bands * (sensors // 8)
     local = (tiles.shape, BF16)
-    sent, series, noisy, *tables = call(
+    sent, series, noisy, *tables, head = call(
         first_kernel,
         "first",
-        [message, rows, ((sensors, 1), F32)] + [(table.shape, BF16) for table in tables],
+        [message, rows, ((sensors, 1), F32)]
+        + [(table.shape, BF16) for table in tables]
+        + [((2, 8, points, freqs), BF16)],
         [(records.shape, F32), ((1, sensors), F32), local, spectra],
         [HBM] * 5,
         *(records, noise.reshape(1, sensors), tiles, *tables),
-        semaphores=[4 + pieces],
+        semaphores=[5 + pieces],
     )
     got = lax.all_to_all(sent, SENS, 0, 0)
     sent, points_0, begin = call(
@@ -525,8 +548,8 @@
         "forward",
         [((half, freqs), F32)] * 2,
         [(wide_shape, F32), flat, rows, local],
-        [SMEM, VMEM, VMEM, HBM, VMEM, VMEM],
-        *(core, weighted_0, prior, tiles, *tables),
+        [SMEM, VMEM, VMEM, VMEM, HBM, VMEM, VMEM],
+        *(core, weighted_0, prior, head, tiles, *tables),
         semaphores=[sensors // 8],
     )
     (sent,) = call(

time: 122 us -> 121 us (level)
  no operation moved by 1% of the time
where the time goes in v6:
time: 121 us; the launch traced here: 120 us
  blocking collectives  88.8 us (73%)
  Pallas kernels  21.6 us (18%)
  starting transfers between devices  7.31 us (6%)
  waiting for transfers between devices  1.87 us (2%)
    all_to_all x2, blocking collectives, on_device(): got = lax.all_to_all(sent, 'z', 0, 0)  36.5 us
    all_to_all x2, blocking collectives, on_device(): got = lax.all_to_all(sent, SENS, 0, 0)  29.3 us
    pallas_call x11, Pallas kernels, call(): pl.pallas_call(kernel, in_specs=specs, out_specs=[VMEM] * len(outs), out_...  21.6 us
    all_to_all x1, blocking collectives, on_device(): weighted_1 = lax.all_to_all(sent, SENS, 0, 0)  11.8 us
    all_to_all x1, blocking collectives, on_device(): weighted_0 = lax.all_to_all(sent, SENS, 0, 0)  11.2 us
    ppermute x3, starting transfers between devices, swap(): return lax.ppermute(block, 'core', [(0, 1), (1, 0)])  7.31 us
  transfers between devices with their start and end apart: 3, of which 2 were waited for; matrix products, arithmetic and copies ran while one was open for 0% of the time, Pallas kernels for 1%

profile of v6, /device:TPU:1, one launch (start us, length us, event | category | flops | bytes accessed | tf_op | source)
XLA Modules:
  0.0 120.3 jit_solution(2554709259885301508)
XLA Ops:
  0.6 0.0 copy-start
  0.7 6.9 %first.1 = (bf16[16,104,128]{2,1,0:T(8,128)(2,1)S(1)}, f32[160,384]{1,0:T(8,128)S(1)}, f32[40,1]{1,0:T(8,128)S(1)}, bf16[384,768]{1,0:T(8,128)(2,1)S(1)}, bf16[3...) custom-call(f32[4,40,383]{2,1,0:T(8,128)} %records, f32[1,40]{1,0:T(1,128)} %bitcast.4, ...), custom_call_target="tpu_custom_call" | custom-call | tf_op jit(solution)/shard_map/first/pallas_call | solution.py:473
  7.6 17.0 %all_to_all.30.got = bf16[16,104,128]{2,1,0:T(8,128)(2,1)S(1)} all-to-all(bf16[16,104,128]{2,1,0:T(8,128)(2,1)S(1)} %get-tuple-element.29), channel_id=1, replica_groups=mesh['y'=4,'x'=4,'z'=8,'core'=2] {'y','x'}, dimensions={0} | all-to-all | bytes 851968 | tf_op jit(solution)/shard_map/all_to_all | solution.py:536
  24.5 0.0 copy-done
  24.5 0.1 weigh.1
  24.6 11.2 %all_to_all.31.weighted = bf16[16,96,128]{2,1,0:T(8,128)(2,1)S(1)} all-to-all(bf16[16,96,128]{2,1,0:T(8,128)(2,1)S(1)} %get-tuple-element.32), channel_id=1, replica_groups=mesh['y'=4,'x'=4,'z'=8,'core'=2] {'y','x'}, dimensions={0} | all-to-all | bytes 786432 | tf_op jit(solution)/shard_map/all_to_all | solution.py:545
  35.8 0.0 copy-start.1
  35.8 5.4 %forward.1 = (f32[80,384]{1,0:T(8,128)S(1)}, f32[80,384]{1,0:T(8,128)S(1)}) custom-call(s32[1]{0:T(128)} %bitcast.core, bf16[16,96,128]{2,1,0:T(8,128)(2,1)S(1)} %all_to_all.31.weighted, f32[64,384]{1,0:T(8,128)S(1)} %copy-done, bf16[2,8,64,384]{3,2,1,0:T(8,128)(2,1)S(1)} %get-tuple-element.34.head, bf16[2,40,64,384]{3,2,1,0:T(8,128)(2,1)} %tiles_in.5, ...), custom_call_target="tpu_custom_call" | custom-call | tf_op jit(solution)/shard_map/forward/pallas_call | solution.py:473
  41.2 3.0 %collective-permute-start = (f32[80,384]{1,0:T(8,128)S(1)}, f32[80,384]{1,0:T(8,128)S(1)}, u32[]{:S(2)}, u32[]{:S(2)}) collective-permute-start(f32[80,384]{1,0:T(8,128)S(1)} %get-tuple-element.38), channel_id=1, source_target_pairs={{0,1},{1,0},{2,3},{3,2},{4,5},{5,4},{6,7},{7,6},{8,9},{9,8},{10,11... | collective-permute-start | bytes 368648 | tf_op jit(solution)/shard_map/ppermute | solution.py:510
  44.3 1.0 collective-permute-done.got
  45.3 24.0 %all_to_all.32.got = bf16[8,80,384]{2,1,0:T(8,128)(2,1)S(1)} all-to-all(bf16[8,80,384]{2,1,0:T(8,128)(2,1)S(1)} %spread.1), channel_id=1, replica_groups=mesh['y'=4,'x'=4,'z'=8,'core'=2] {'z'}, dimensions={0} | all-to-all | bytes 983040 | tf_op jit(solution)/shard_map/all_to_all | solution.py:563
  69.3 0.1 gather.1.mine
  69.3 1.8 %collective-permute-start.1 = (f32[80,384]{1,0:T(8,128)S(1)}, f32[80,384]{1,0:T(8,128)S(1)}, u32[]{:S(2)}, u32[]{:S(2)}) collective-permute-start(f32[80,384]{1,0:T(8,128)S(1)} %gather.1.mine), channel_id=1, source_target_pairs={{0,1},{1,0},{2,3},{3,2},{4,5},{5,4},{6,7},{7,6},{8,9},{9,8},{10,11... | collective-permute-start | bytes 368648 | tf_op jit(solution)/shard_map/ppermute | solution.py:510
  71.2 0.0 copy-done.1
  71.2 1.0 site_0.1
  72.1 0.0 collective-permute-done.1.theirs
  72.1 5.9 %second.1 = (bf16[16,104,128]{2,1,0:T(8,128)(2,1)S(1)}, f32[160,384]{1,0:T(8,128)S(1)}, f32[8,128]{1,0:T(8,128)S(1)}) custom-call(s32[1]{0:T(128)} %bitcast.core, f32[80,384]{1,0:T(8,128)S(1)} %gather.1.mine, f32[80,384]{1,0:T(8,128)S(1)} %collective-permute-done.1.theirs, f32[160,384]{1,0:T(8,128)S(1)} %get-tuple-element.44.series, ...), custom_call_target="tpu_custom_call" | custom-call | tf_op jit(solution)/shard_map/second/pallas_call | solution.py:473
  78.0 12.3 %all_to_all.33.got = bf16[16,104,128]{2,1,0:T(8,128)(2,1)S(1)} all-to-all(bf16[16,104,128]{2,1,0:T(8,128)(2,1)S(1)} %get-tuple-element.47), channel_id=1, replica_groups=mesh['y'=4,'x'=4,'z'=8,'core'=2] {'y','x'}, dimensions={0} | all-to-all | bytes 851968 | tf_op jit(solution)/shard_map/all_to_all | solution.py:577
  90.4 0.2 weigh_next.1
  90.6 11.8 %all_to_all.34.weighted = bf16[16,96,128]{2,1,0:T(8,128)(2,1)S(1)} all-to-all(bf16[16,96,128]{2,1,0:T(8,128)(2,1)S(1)} %get-tuple-element.50), channel_id=1, replica_groups=mesh['y'=4,'x'=4,'z'=8,'core'=2] {'y','x'}, dimensions={0} | all-to-all | bytes 786432 | tf_op jit(solution)/shard_map/all_to_all | solution.py:586
  102.4 1.0 site_1.1
  103.4 2.4 %collective-permute-start.2 = (f32[32,384]{1,0:T(8,128)S(1)}, f32[32,384]{1,0:T(8,128)S(1)}, u32[]{:S(2)}, u32[]{:S(2)}) collective-permute-start(f32[32,384]{1,0:T(8,128)S(1)} %pad_maximum_fusion.mine), channel_id=1, source_target_pairs={{0,1},{1,0},{2,3},{3,2},{4,5},{5,4},{6,7},{7,6},{8,9},{9,8},{10,11... | collective-permute-start | bytes 147464 | tf_op jit(solution)/shard_map/ppermute | solution.py:510
  105.8 0.9 collective-permute-done.2.got
  106.7 12.5 %all_to_all.35.got = bf16[8,32,384]{2,1,0:T(8,128)(2,1)S(1)} all-to-all(bf16[8,32,384]{2,1,0:T(8,128)(2,1)S(1)} %spread_sites.1), channel_id=1, replica_groups=mesh['y'=4,'x'=4,'z'=8,'core'=2] {'z'}, dimensions={0} | all-to-all | bytes 393216 | tf_op jit(solution)/shard_map/all_to_all | solution.py:597
  119.2 1.0 last.1
  (3 shorter events, 0.1 us)
Async XLA Ops:
  0.6 23.9 %copy-start = (f32[64,384]{1,0:T(8,128)S(1)}, f32[64,384]{1,0:T(8,128)}, u32[]{:S(2)}) copy-start(f32[64,384]{1,0:T(8,128)} %prior.4) | copy-start | bytes 294916
  35.8 35.4 %copy-start.1 = (bf16[2,4,64,384]{3,2,1,0:T(8,128)(2,1)S(1)}, bf16[2,4,64,384]{3,2,1,0:T(8,128)(2,1)}, u32[]{:S(2)}) copy-start(bf16[2,4,64,384]{3,2,1,0:T(8,128)(2,1)} %tiles.1) | copy-start | bytes 1179652
  41.2 4.0 %collective-permute-start = (f32[80,384]{1,0:T(8,128)S(1)}, f32[80,384]{1,0:T(8,128)S(1)}, u32[]{:S(2)}, u32[]{:S(2)}) collective-permute-start(f32[80,384]{1,0:T(8,128)S(1)} %get-tuple-element.38), channel_id=1, source_target_pairs={{0,1},{1,0},{2,3},{3,2},{4,5},{5,4},{6,7},{7,6},{8,9},{9,8},{10,11... | collective-permute-start | bytes 368648 | tf_op jit(solution)/shard_map/ppermute | solution.py:510
  69.3 2.8 %collective-permute-start.1 = (f32[80,384]{1,0:T(8,128)S(1)}, f32[80,384]{1,0:T(8,128)S(1)}, u32[]{:S(2)}, u32[]{:S(2)}) collective-permute-start(f32[80,384]{1,0:T(8,128)S(1)} %gather.1.mine), channel_id=1, source_target_pairs={{0,1},{1,0},{2,3},{3,2},{4,5},{5,4},{6,7},{7,6},{8,9},{9,8},{10,11... | collective-permute-start | bytes 368648 | tf_op jit(solution)/shard_map/ppermute | solution.py:510
  103.4 3.3 %collective-permute-start.2 = (f32[32,384]{1,0:T(8,128)S(1)}, f32[32,384]{1,0:T(8,128)S(1)}, u32[]{:S(2)}, u32[]{:S(2)}) collective-permute-start(f32[32,384]{1,0:T(8,128)S(1)} %pad_maximum_fusion.mine), channel_id=1, source_target_pairs={{0,1},{1,0},{2,3},{3,2},{4,5},{5,4},{6,7},{7,6},{8,9},{9,8},{10,11... | collective-permute-start | bytes 147464 | tf_op jit(solution)/shard_map/ppermute | solution.py:510
